TPU v7x, 512 devices: a whole 4x4x16 slice. The times are simulated.
512 devices in a mesh: leaf: 128 (over z, y, core), level: 4 (over x).
Axes of the slice: x: 4, y: 4, z: 16, core: 2. Of those that a mesh axis runs over, the one named last changes fastest.
Arguments:
- points_x: bfloat16 [256, 262144], P(None, ('leaf', 'level')), may hold values from -6 to 6
- leaf_basis: bfloat16 [512, 512, 256], P(('leaf', 'level')), may hold values from -0.25 to 0.25
- near_tiles: bfloat16 [512, 4, 512, 512], P(('leaf', 'level')), may hold values from -0.25 to 0.25
- near_cols: int32 [512, 4], P(('leaf', 'level')), may hold values from 0 to 11, as said below
- near_count: int32 [512], P(('leaf', 'level')), may hold values from 3 to 4, as said below
- transfer: bfloat16 [2, 256, 256], replicated, may hold values from -0.3125 to 0.3125
- coupling: bfloat16 [6, 2, 256, 256], replicated, may hold values from -0.375 to 0.375
- couple_mask: int32 [6, 128, 2], replicated, may hold values 0 or 1
Outputs:
- kernel_product: bfloat16 [256, 262144], P(None, ('leaf', 'level'))
Inputs may be any that keep to these rules, and one draw needn't show every extreme that they name: Slots 0, 1 and 2 of leaf L name L itself, L - 1 and L + 1 (near_cols 4 + L mod 4, one less, one more); slot 3 names any leaf of the previous, own or next group; some leaf's slot 3 names 0 and some names 11. The live slots of a leaf are its first near_count slots; in every draw some leaf has 3 and some has 4 live slots.
All inputs are finite; a program needn't handle non-finite values.
Results may differ from a plain program's by a relative error of at most 0.015.
Values may be sent and summed in bfloat16 or wider, within the bound.
A program may use at most 64 MiB of HBM per device.

v0:
```python
from functools import partial

import jax
import jax.numpy as jnp
from jax import lax
from jax.sharding import PartitionSpec as P


def shifted(value, axis, steps):
    count = lax.axis_size(axis)
    leading, last = (max(0, -steps), min(count, count - steps))
    return lax.ppermute(value, axis, [(source, source + steps) for source in range(leading, last)])


def with_halo(block, sides, width):
    for axis, dim in sides:
        count = lax.axis_size(axis)
        forward = [(i, i + 1) for i in range(count - 1)]
        backward = [(target, source) for source, target in forward]
        low = lax.ppermute(
            lax.slice_in_dim(block, block.shape[dim] - width, None, axis=dim), axis, forward
        )
        high = lax.ppermute(lax.slice_in_dim(block, 0, width, axis=dim), axis, backward)
        block = jnp.concatenate([low, block, high], axis=dim)
    return block


def in_one_piece(arrays, axis, dim, along):
    widths = [a.shape[along] for a in arrays]
    both = jnp.concatenate(arrays, axis=along)
    whole = lax.all_gather(both, axis, axis=dim, tiled=True)
    return tuple(jnp.split(whole, [sum(widths[:k]) for k in range(1, len(widths))], axis=along))


def swapped(block, axis, distance):
    count = lax.axis_size(axis)
    route = []
    for low in range(count):
        high = low | 1 << distance
        if high != low and high < count:
            route += [(low, high), (high, low)]
    return lax.ppermute(block, axis, route)


def pair_sum(lower_coef, upper_coef, transfer):
    summed = jnp.dot(lower_coef, transfer[0], preferred_element_type=jnp.float32)
    summed = summed + jnp.dot(upper_coef, transfer[1], preferred_element_type=jnp.float32)
    return summed.astype(jnp.bfloat16)


def down_one(fields, matrix):
    return lax.dot_general(
        fields, matrix, (((1,), (1,)), ((), ())), preferred_element_type=jnp.float32
    )


def partner(coefs, distance):
    return shifted(coefs, "leaf", distance)


def add_tile(column_x, tile_block, running):
    return running + jnp.dot(column_x, tile_block, preferred_element_type=jnp.float32)


def keep_same(running):
    return running


def per_device(
    points_x, leaf_basis, near_tiles, near_cols, near_count, transfer, coupling, couple_mask
):
    group_size = lax.axis_size("level")
    leaf_count = lax.axis_size("leaf")
    group_pos = lax.axis_index("level")
    leaf_pos = lax.axis_index("leaf")
    vectors, points = points_x.shape
    leaf_map = leaf_basis[0]
    slot_count = near_tiles.shape[1]
    levels = coupling.shape[0]
    group_bits = group_size.bit_length() - 1
    leaf_bits = leaf_count.bit_length() - 1
    active = min(levels, leaf_bits + 1)
    leaf_coef = jnp.dot(points_x, leaf_map, preferred_element_type=jnp.float32).astype(jnp.bfloat16)
    padded = with_halo(points_x, (("leaf", 1),), points)
    left_g, own_g, right_g, group_coef = (
        *in_one_piece((padded[:, :points], points_x, padded[:, 2 * points :]), "level", 1, 0),
        lax.all_gather(leaf_coef[None], "level", axis=0, tiled=True),
    )
    window_x = jnp.concatenate([left_g, own_g, right_g], axis=1)
    level_coefs = [group_coef[member] for member in range(group_size)]
    while len(level_coefs) > 1:
        level_coefs = [
            pair_sum(level_coefs[2 * pair_idx], level_coefs[2 * pair_idx + 1], transfer)
            for pair_idx in range(len(level_coefs) // 2)
        ]
    top_coef = level_coefs[0]
    vec_share = vectors // group_size
    top_coef = lax.dynamic_slice_in_dim(top_coef, group_pos * vec_share, vec_share, 0)
    coarse = [top_coef]
    for level_idx in range(1, active):
        bit_num = level_idx - 1
        current = coarse[-1]
        own_side = leaf_pos >> bit_num & 1
        is_upper = own_side == 1
        partner_coef = swapped(current, "leaf", bit_num)
        lower_coef = jnp.where(is_upper, partner_coef, current)
        upper_coef = jnp.where(is_upper, current, partner_coef)
        coarse.append(pair_sum(lower_coef, upper_coef, transfer))
    couplings = []
    for level_idx in range(active):
        stride = 1 << level_idx
        cluster = leaf_pos >> level_idx
        coupled = jnp.zeros(coarse[level_idx].shape, jnp.float32)
        for pick_idx, offset in enumerate((2, 3)):
            matrix = coupling[level_idx, pick_idx]
            ahead_coef = partner(coarse[level_idx], -offset * stride)
            behind = partner(coarse[level_idx], offset * stride)
            ahead_mask = couple_mask[level_idx, cluster, pick_idx].astype(jnp.float32)
            behind_mask = couple_mask[level_idx, jnp.maximum(cluster - offset, 0), pick_idx].astype(
                jnp.float32
            )
            coupled = coupled + ahead_mask * jnp.dot(
                ahead_coef, matrix, preferred_element_type=jnp.float32
            )
            coupled = coupled + behind_mask * down_one(behind, matrix)
        couplings.append(coupled)
    fields = couplings[active - 1].astype(jnp.bfloat16)
    for level_idx in range(active - 2, -1, -1):
        child_side = leaf_pos >> level_idx & 1
        fields = (down_one(fields, transfer[child_side]) + couplings[level_idx]).astype(
            jnp.bfloat16
        )
    fields = lax.all_gather(fields, "level", axis=0, tiled=True)
    for bit_num in range(group_bits - 1, -1, -1):
        child_side = group_pos >> bit_num & 1
        fields = down_one(fields, transfer[child_side]).astype(jnp.bfloat16)
    far_field = down_one(fields, leaf_map)
    tile_count = near_count[0]
    near_field = far_field
    for slot_idx in range(slot_count):
        column_x = lax.dynamic_slice_in_dim(window_x, near_cols[0, slot_idx] * points, points, 1)
        near_field = lax.cond(
            slot_idx < tile_count,
            partial(add_tile, column_x, near_tiles[0, slot_idx]),
            keep_same,
            near_field,
        )
    return near_field.astype(jnp.bfloat16)


def solution(mesh):
    in_specs = (
        P(None, ("leaf", "level")),
        P(("leaf", "level"), None, None),
        P(("leaf", "level"), None, None, None),
        P(("leaf", "level"), None),
        P(("leaf", "level")),
        P(),
        P(),
        P(),
    )
    out_specs = P(None, ("leaf", "level"))
    return jax.shard_map(
        per_device, mesh=mesh, in_specs=in_specs, out_specs=out_specs, check_vma=False
    )
```

profile of v0, /device:TPU:2, one launch (start us, length us, event | category | flops | bytes accessed | tf_op | source)
XLA Modules:
  0.0 276.6 jit_solution(5910400586805205190)
XLA Ops:
  6.5 2.6 collective-permute-start.29
  11.6 15.7 %all-gather = bf16[1024,256]{1,0:T(8,128)(2,1)S(1)} all-gather(bf16[256,256]{1,0:T(8,128)(2,1)S(1)} %convolution_convert_fusion), channel_id=2, replica_groups=mesh['leaf'=128,'level'=4] {'level'}, dimensions={0}, use_global_device_ids=true | all-gather | bytes 655360 | tf_op jit(solution)/shard_map/all_gather | solution.py:87
  29.3 1.3 collective-permute-start.27
  30.6 3.2 %collective-permute-start.26 = (bf16[64,256]{1,0:T(8,128)(2,1)S(1)}, bf16[64,256]{1,0:T(8,128)(2,1)S(1)}, u32[]{:S(2)}, u32[]{:S(2)}) collective-permute-start(bf16[64,256]{1,0:T(8,128)(2,1)S(1)} %fusion.166), channel_id=1, source_target_pairs={{0,8},{4,12},{8,16},{12,20},{16,24},{20,28},{24,32},{28,36},{32,40... | collective-permute-start | bytes 98312 | tf_op jit(solution)/shard_map/ppermute | solution.py:12
  33.8 3.1 %collective-permute-start = (bf16[64,256]{1,0:T(8,128)(2,1)S(1)}, bf16[64,256]{1,0:T(8,128)(2,1)S(1)}, u32[]{:S(2)}, u32[]{:S(2)}) collective-permute-start(bf16[64,256]{1,0:T(8,128)(2,1)S(1)} %fusion.166), channel_id=1, source_target_pairs={{0,4},{4,0},{8,12},{12,8},{16,20},{20,16},{24,28},{28,24},{32,36},... | collective-permute-start | bytes 98312 | tf_op jit(solution)/shard_map/ppermute | solution.py:42
  55.8 1.3 collective-permute-start.25
  57.5 3.9 %collective-permute-start.28 = (bf16[64,256]{1,0:T(8,128)(2,1)S(1)}, bf16[64,256]{1,0:T(8,128)(2,1)S(1)}, u32[]{:S(2)}, u32[]{:S(2)}) collective-permute-start(bf16[64,256]{1,0:T(8,128)(2,1)S(1)} %fusion.166), channel_id=1, source_target_pairs={{0,12},{4,16},{8,20},{12,24},{16,28},{20,32},{24,36},{28,40},{32,4... | collective-permute-start | bytes 98312 | tf_op jit(solution)/shard_map/ppermute | solution.py:12
  61.5 8.9 %collective-permute-start.24 = (bf16[64,256]{1,0:T(8,128)(2,1)S(1)}, bf16[64,256]{1,0:T(8,128)(2,1)S(1)}, u32[]{:S(2)}, u32[]{:S(2)}) collective-permute-start(bf16[64,256]{1,0:T(8,128)(2,1)S(1)} %fusion.44), channel_id=1, source_target_pairs={{0,24},{4,28},{8,32},{12,36},{16,40},{20,44},{24,48},{28,52},{32,5... | collective-permute-start | bytes 98312 | tf_op jit(solution)/shard_map/ppermute | solution.py:12
  70.6 1.9 collective-permute-start.1
  72.7 3.7 %collective-permute-done.1 = bf16[64,256]{1,0:T(8,128)(2,1)S(1)} collective-permute-done((bf16[64,256]{1,0:T(8,128)(2,1)S(1)}, bf16[64,256]{1,0:T(8,128)(2,1)S(1)}, u32[]{:S(2)}, u32[]{:S(2)}) %collective-permute-start.1) | collective-permute-done | bytes 32800 | tf_op jit(solution)/shard_map/ppermute | solution.py:42
  76.4 1.3 collective-permute-start.23
  78.0 1.4 collective-permute-start.22
  79.6 3.9 %collective-permute-done.23 = bf16[64,256]{1,0:T(8,128)(2,1)S(1)} collective-permute-done((bf16[64,256]{1,0:T(8,128)(2,1)S(1)}, bf16[64,256]{1,0:T(8,128)(2,1)S(1)}, u32[]{:S(2)}, u32[]{:S(2)}) %collective-permute-start.23) | collective-permute-done | bytes 32800 | tf_op jit(solution)/shard_map/ppermute | solution.py:12
  84.9 6.1 %collective-permute-start.2 = (bf16[64,256]{1,0:T(8,128)(2,1)S(1)}, bf16[64,256]{1,0:T(8,128)(2,1)S(1)}, u32[]{:S(2)}, u32[]{:S(2)}) collective-permute-start(bf16[64,256]{1,0:T(8,128)(2,1)S(1)} %fusion.45), channel_id=1, source_target_pairs={{0,16},{16,0},{4,20},{20,4},{8,24},{24,8},{12,28},{28,12},{32,48},... | collective-permute-start | bytes 98312 | tf_op jit(solution)/shard_map/ppermute | solution.py:42
  91.1 1.7 collective-permute-done.2
  92.8 6.8 %collective-permute-start.20 = (bf16[64,256]{1,0:T(8,128)(2,1)S(1)}, bf16[64,256]{1,0:T(8,128)(2,1)S(1)}, u32[]{:S(2)}, u32[]{:S(2)}) collective-permute-start(bf16[64,256]{1,0:T(8,128)(2,1)S(1)} %fusion.45), channel_id=1, source_target_pairs={{0,48},{4,52},{8,56},{12,60},{16,64},{20,68},{24,72},{28,76},{32,8... | collective-permute-start | bytes 98312 | tf_op jit(solution)/shard_map/ppermute | solution.py:12
  99.8 1.4 collective-permute-done.20
  102.6 10.0 %collective-permute-done.19 = bf16[64,256]{1,0:T(8,128)(2,1)S(1)} collective-permute-done((bf16[64,256]{1,0:T(8,128)(2,1)S(1)}, bf16[64,256]{1,0:T(8,128)(2,1)S(1)}, u32[]{:S(2)}, u32[]{:S(2)}) %collective-permute-start.19) | collective-permute-done | bytes 32800 | tf_op jit(solution)/shard_map/ppermute | solution.py:12
  112.7 5.8 %collective-permute-start.18 = (bf16[64,256]{1,0:T(8,128)(2,1)S(1)}, bf16[64,256]{1,0:T(8,128)(2,1)S(1)}, u32[]{:S(2)}, u32[]{:S(2)}) collective-permute-start(bf16[64,256]{1,0:T(8,128)(2,1)S(1)} %fusion.45), channel_id=1, source_target_pairs={{0,32},{4,36},{8,40},{12,44},{16,48},{20,52},{24,56},{28,60},{32,6... | collective-permute-start | bytes 98312 | tf_op jit(solution)/shard_map/ppermute | solution.py:12
  118.6 1.4 collective-permute-done.18
  121.7 10.8 %collective-permute-start.16 = (bf16[64,256]{1,0:T(8,128)(2,1)S(1)}, bf16[64,256]{1,0:T(8,128)(2,1)S(1)}, u32[]{:S(2)}, u32[]{:S(2)}) collective-permute-start(bf16[64,256]{1,0:T(8,128)(2,1)S(1)} %fusion.46), channel_id=1, source_target_pairs={{0,96},{4,100},{8,104},{12,108},{16,112},{20,116},{24,120},{28,124... | collective-permute-start | bytes 98312 | tf_op jit(solution)/shard_map/ppermute | solution.py:12
  132.5 5.4 %collective-permute-start.3 = (bf16[64,256]{1,0:T(8,128)(2,1)S(1)}, bf16[64,256]{1,0:T(8,128)(2,1)S(1)}, u32[]{:S(2)}, u32[]{:S(2)}) collective-permute-start(bf16[64,256]{1,0:T(8,128)(2,1)S(1)} %fusion.46), channel_id=1, source_target_pairs={{0,32},{32,0},{4,36},{36,4},{8,40},{40,8},{12,44},{44,12},{16,48},... | collective-permute-start | bytes 98312 | tf_op jit(solution)/shard_map/ppermute | solution.py:42
  138.0 2.0 pad_maximum_fusion.1
  140.0 1.3 collective-permute-start.15
  141.6 5.2 %collective-permute-start.14 = (bf16[64,256]{1,0:T(8,128)(2,1)S(1)}, bf16[64,256]{1,0:T(8,128)(2,1)S(1)}, u32[]{:S(2)}, u32[]{:S(2)}) collective-permute-start(bf16[64,256]{1,0:T(8,128)(2,1)S(1)} %fusion.46), channel_id=1, source_target_pairs={{0,64},{4,68},{8,72},{12,76},{16,80},{20,84},{24,88},{28,92},{32,9... | collective-permute-start | bytes 98312 | tf_op jit(solution)/shard_map/ppermute | solution.py:12
  147.6 1.3 collective-permute-start.13
  149.0 7.8 %collective-permute-start.4 = (bf16[64,256]{1,0:T(8,128)(2,1)S(1)}, bf16[64,256]{1,0:T(8,128)(2,1)S(1)}, u32[]{:S(2)}, u32[]{:S(2)}) collective-permute-start(bf16[64,256]{1,0:T(8,128)(2,1)S(1)} %fusion.47), channel_id=1, source_target_pairs={{0,64},{64,0},{4,68},{68,4},{8,72},{72,8},{12,76},{76,12},{16,80},... | collective-permute-start | bytes 98312 | tf_op jit(solution)/shard_map/ppermute | solution.py:42
  157.0 2.1 collective-permute-done.4
  159.0 10.5 %collective-permute-start.12 = (bf16[64,256]{1,0:T(8,128)(2,1)S(1)}, bf16[64,256]{1,0:T(8,128)(2,1)S(1)}, u32[]{:S(2)}, u32[]{:S(2)}) collective-permute-start(bf16[64,256]{1,0:T(8,128)(2,1)S(1)} %fusion.47), channel_id=1, source_target_pairs={{0,192},{4,196},{8,200},{12,204},{16,208},{20,212},{24,216},{28,22... | collective-permute-start | bytes 98312 | tf_op jit(solution)/shard_map/ppermute | solution.py:12
  172.6 10.4 %collective-permute-done.11 = bf16[64,256]{1,0:T(8,128)(2,1)S(1)} collective-permute-done((bf16[64,256]{1,0:T(8,128)(2,1)S(1)}, bf16[64,256]{1,0:T(8,128)(2,1)S(1)}, u32[]{:S(2)}, u32[]{:S(2)}) %collective-permute-start.11) | collective-permute-done | bytes 32800 | tf_op jit(solution)/shard_map/ppermute | solution.py:12
  182.9 5.2 %collective-permute-start.10 = (bf16[64,256]{1,0:T(8,128)(2,1)S(1)}, bf16[64,256]{1,0:T(8,128)(2,1)S(1)}, u32[]{:S(2)}, u32[]{:S(2)}) collective-permute-start(bf16[64,256]{1,0:T(8,128)(2,1)S(1)} %fusion.47), channel_id=1, source_target_pairs={{0,128},{4,132},{8,136},{12,140},{16,144},{20,148},{24,152},{28,15... | collective-permute-start | bytes 98312 | tf_op jit(solution)/shard_map/ppermute | solution.py:12
  188.3 1.4 collective-permute-done.10
  189.7 12.0 %collective-permute-start.8 = (bf16[64,256]{1,0:T(8,128)(2,1)S(1)}, bf16[64,256]{1,0:T(8,128)(2,1)S(1)}, u32[]{:S(2)}, u32[]{:S(2)}) collective-permute-start(bf16[64,256]{1,0:T(8,128)(2,1)S(1)} %fusion.48), channel_id=1, source_target_pairs={{0,384},{4,388},{8,392},{12,396},{16,400},{20,404},{24,408},{28,41... | collective-permute-start | bytes 98312 | tf_op jit(solution)/shard_map/ppermute | solution.py:12
  201.9 1.4 collective-permute-done.8
  204.7 8.3 %collective-permute-done.7 = bf16[64,256]{1,0:T(8,128)(2,1)S(1)} collective-permute-done((bf16[64,256]{1,0:T(8,128)(2,1)S(1)}, bf16[64,256]{1,0:T(8,128)(2,1)S(1)}, u32[]{:S(2)}, u32[]{:S(2)}) %collective-permute-start.7) | collective-permute-done | bytes 32800 | tf_op jit(solution)/shard_map/ppermute | solution.py:12
  214.4 1.4 collective-permute-done.6
  217.3 13.1 %collective-permute-done.5 = bf16[64,256]{1,0:T(8,128)(2,1)S(1)} collective-permute-done((bf16[64,256]{1,0:T(8,128)(2,1)S(1)}, bf16[64,256]{1,0:T(8,128)(2,1)S(1)}, u32[]{:S(2)}, u32[]{:S(2)}) %collective-permute-start.5) | collective-permute-done | bytes 32800 | tf_op jit(solution)/shard_map/ppermute | solution.py:12
  232.7 7.6 %collective-permute-done.9 = bf16[64,256]{1,0:T(8,128)(2,1)} collective-permute-done((bf16[64,256]{1,0:T(8,128)(2,1)S(1)}, bf16[64,256]{1,0:T(8,128)(2,1)}, u32[]{:S(2)}, u32[]{:S(2)}) %collective-permute-start.9) | collective-permute-done | bytes 32800 | tf_op jit(solution)/shard_map/ppermute | solution.py:12
  244.7 12.0 %all_gather.10 = bf16[256,256]{1,0:T(8,128)(2,1)S(1)} all-gather(bf16[64,256]{1,0:T(8,128)(2,1)S(1)} %fusion.49), channel_id=1, replica_groups=mesh['leaf'=128,'level'=4] {'level'}, dimensions={0}, use_global_device_ids=true | all-gather | bytes 163840 | tf_op jit(solution)/shard_map/all_gather | solution.py:133
  257.4 2.2 fusion.217
  259.7 1.8 pad_maximum_fusion
  262.4 1.3 conditional.7
  262.4 1.3 convolution_add_fusion.1
  263.7 1.4 conditional.8
  263.7 1.3 convolution_add_fusion.2
  265.1 1.4 conditional.9
  265.1 1.3 convolution_add_fusion.3
  266.4 2.5 conditional.11
  (92 shorter events, 32.1 us)
Async XLA Ops:
  6.5 3.9 %copy-start = (bf16[1,512,256]{2,1,0:T(8,128)(2,1)S(1)}, bf16[1,512,256]{2,1,0:T(8,128)(2,1)}, u32[]{:S(2)}) copy-start(bf16[1,512,256]{2,1,0:T(8,128)(2,1)} %param.17) | copy-start | bytes 786436
  6.5 21.8 %copy-start.1 = (bf16[2,256,256]{2,1,0:T(8,128)(2,1)S(1)}, bf16[2,256,256]{2,1,0:T(8,128)(2,1)}, u32[]{:S(2)}) copy-start(bf16[2,256,256]{2,1,0:T(8,128)(2,1)} %param.21) | copy-start | bytes 786436
  6.5 250.8 %all-gather.3.cloned.1.call-start = ((), (), s32[]{:S(2)}) async-start(), calls=%async_computation | async-start | bytes 3932160 | tf_op jit(solution)/shard_map/all_gather | solution.py:31
  6.5 115.1 %collective-permute-start.29 = (bf16[256,512]{1,0:T(8,128)(2,1)}, bf16[256,512]{1,0:T(8,128)(2,1)}, u32[]{:S(2)}, u32[]{:S(2)}) collective-permute-start(bf16[256,512]{1,0:T(8,128)(2,1)} %param.16), channel_id=1, source_target_pairs={{0,4},{4,8},{8,12},{12,16},{16,20},{20,24},{24,28},{28,32},{32,36}... | collective-permute-start | bytes 786440 | tf_op jit(solution)/shard_map/ppermute | solution.py:20
  9.1 123.4 %collective-permute-start.30 = (bf16[256,512]{1,0:T(8,128)(2,1)}, bf16[256,512]{1,0:T(8,128)(2,1)}, u32[]{:S(2)}, u32[]{:S(2)}) collective-permute-start(bf16[256,512]{1,0:T(8,128)(2,1)} %param.16), channel_id=1, source_target_pairs={{4,0},{8,4},{12,8},{16,12},{20,16},{24,20},{28,24},{32,28},{36,32}... | collective-permute-start | bytes 786440 | tf_op jit(solution)/shard_map/ppermute | solution.py:23
  27.3 9.6 %copy-start.7 = (s32[1,4]{1,0:T(1,128)S(1)}, s32[1,4]{1,0:T(1,128)}, u32[]{:S(2)}) copy-start(s32[1,4]{1,0:T(1,128)} %param.19) | copy-start | bytes 52
  27.3 12.8 %copy-start.6 = (s32[6,128,2]{1,2,0:T(2,128)S(1)}, s32[6,128,2]{1,2,0:T(2,128)}, u32[]{:S(2)}) copy-start(s32[6,128,2]{1,2,0:T(2,128)} %param.23) | copy-start | bytes 18436
  28.6 32.8 %copy-start.2 = (bf16[6,2,256,256]{3,2,1,0:T(8,128)(2,1)S(1)}, bf16[6,2,256,256]{3,2,1,0:T(8,128)(2,1)}, u32[]{:S(2)}) copy-start(bf16[6,2,256,256]{3,2,1,0:T(8,128)(2,1)} %param.22) | copy-start | bytes 4718596
  29.3 28.2 %collective-permute-start.27 = (bf16[64,256]{1,0:T(8,128)(2,1)S(1)}, bf16[64,256]{1,0:T(8,128)(2,1)S(1)}, u32[]{:S(2)}, u32[]{:S(2)}) collective-permute-start(bf16[64,256]{1,0:T(8,128)(2,1)S(1)} %fusion.166), channel_id=1, source_target_pairs={{12,0},{16,4},{20,8},{24,12},{28,16},{32,20},{36,24},{40,28},{44,3... | collective-permute-start | bytes 98312 | tf_op jit(solution)/shard_map/ppermute | solution.py:12
  30.6 30.9 %collective-permute-start.26 = (bf16[64,256]{1,0:T(8,128)(2,1)S(1)}, bf16[64,256]{1,0:T(8,128)(2,1)S(1)}, u32[]{:S(2)}, u32[]{:S(2)}) collective-permute-start(bf16[64,256]{1,0:T(8,128)(2,1)S(1)} %fusion.166), channel_id=1, source_target_pairs={{0,8},{4,12},{8,16},{12,20},{16,24},{20,28},{24,32},{28,36},{32,40... | collective-permute-start | bytes 98312 | tf_op jit(solution)/shard_map/ppermute | solution.py:12
  33.8 22.0 %collective-permute-start = (bf16[64,256]{1,0:T(8,128)(2,1)S(1)}, bf16[64,256]{1,0:T(8,128)(2,1)S(1)}, u32[]{:S(2)}, u32[]{:S(2)}) collective-permute-start(bf16[64,256]{1,0:T(8,128)(2,1)S(1)} %fusion.166), channel_id=1, source_target_pairs={{0,4},{4,0},{8,12},{12,8},{16,20},{20,16},{24,28},{28,24},{32,36},... | collective-permute-start | bytes 98312 | tf_op jit(solution)/shard_map/ppermute | solution.py:42
  55.8 188.7 %collective-permute-start.25 = (bf16[64,256]{1,0:T(8,128)(2,1)S(1)}, bf16[64,256]{1,0:T(8,128)(2,1)S(1)}, u32[]{:S(2)}, u32[]{:S(2)}) collective-permute-start(bf16[64,256]{1,0:T(8,128)(2,1)S(1)} %fusion.166), channel_id=1, source_target_pairs={{8,0},{12,4},{16,8},{20,12},{24,16},{28,20},{32,24},{36,28},{40,32... | collective-permute-start | bytes 98312 | tf_op jit(solution)/shard_map/ppermute | solution.py:12
  57.5 13.2 %collective-permute-start.28 = (bf16[64,256]{1,0:T(8,128)(2,1)S(1)}, bf16[64,256]{1,0:T(8,128)(2,1)S(1)}, u32[]{:S(2)}, u32[]{:S(2)}) collective-permute-start(bf16[64,256]{1,0:T(8,128)(2,1)S(1)} %fusion.166), channel_id=1, source_target_pairs={{0,12},{4,16},{8,20},{12,24},{16,28},{20,32},{24,36},{28,40},{32,4... | collective-permute-start | bytes 98312 | tf_op jit(solution)/shard_map/ppermute | solution.py:12
  61.4 76.6 %copy-start.4 = (bf16[256,512]{1,0:T(8,128)(2,1)S(1)}, bf16[256,512]{1,0:T(8,128)(2,1)}, u32[]{:S(2)}) copy-start(bf16[256,512]{1,0:T(8,128)(2,1)} %param.16) | copy-start | bytes 786436
  61.5 16.5 %collective-permute-start.24 = (bf16[64,256]{1,0:T(8,128)(2,1)S(1)}, bf16[64,256]{1,0:T(8,128)(2,1)S(1)}, u32[]{:S(2)}, u32[]{:S(2)}) collective-permute-start(bf16[64,256]{1,0:T(8,128)(2,1)S(1)} %fusion.44), channel_id=1, source_target_pairs={{0,24},{4,28},{8,32},{12,36},{16,40},{20,44},{24,48},{28,52},{32,5... | collective-permute-start | bytes 98312 | tf_op jit(solution)/shard_map/ppermute | solution.py:12
  70.6 5.8 %collective-permute-start.1 = (bf16[64,256]{1,0:T(8,128)(2,1)S(1)}, bf16[64,256]{1,0:T(8,128)(2,1)S(1)}, u32[]{:S(2)}, u32[]{:S(2)}) collective-permute-start(bf16[64,256]{1,0:T(8,128)(2,1)S(1)} %fusion.44), channel_id=1, source_target_pairs={{0,8},{8,0},{4,12},{12,4},{16,24},{24,16},{20,28},{28,20},{32,40},... | collective-permute-start | bytes 98312 | tf_op jit(solution)/shard_map/ppermute | solution.py:42
  76.4 7.0 %collective-permute-start.23 = (bf16[64,256]{1,0:T(8,128)(2,1)S(1)}, bf16[64,256]{1,0:T(8,128)(2,1)S(1)}, u32[]{:S(2)}, u32[]{:S(2)}) collective-permute-start(bf16[64,256]{1,0:T(8,128)(2,1)S(1)} %fusion.44), channel_id=1, source_target_pairs={{24,0},{28,4},{32,8},{36,12},{40,16},{44,20},{48,24},{52,28},{56,3... | collective-permute-start | bytes 98312 | tf_op jit(solution)/shard_map/ppermute | solution.py:12
  78.0 6.8 %collective-permute-start.22 = (bf16[64,256]{1,0:T(8,128)(2,1)S(1)}, bf16[64,256]{1,0:T(8,128)(2,1)S(1)}, u32[]{:S(2)}, u32[]{:S(2)}) collective-permute-start(bf16[64,256]{1,0:T(8,128)(2,1)S(1)} %fusion.44), channel_id=1, source_target_pairs={{0,16},{4,20},{8,24},{12,28},{16,32},{20,36},{24,40},{28,44},{32,4... | collective-permute-start | bytes 98312 | tf_op jit(solution)/shard_map/ppermute | solution.py:12
  83.4 160.0 %collective-permute-start.21 = (bf16[64,256]{1,0:T(8,128)(2,1)S(1)}, bf16[64,256]{1,0:T(8,128)(2,1)}, u32[]{:S(2)}, u32[]{:S(2)}) collective-permute-start(bf16[64,256]{1,0:T(8,128)(2,1)S(1)} %fusion.44), channel_id=1, source_target_pairs={{16,0},{20,4},{24,8},{28,12},{32,16},{36,20},{40,24},{44,28},{48,3... | collective-permute-start | bytes 98312 | tf_op jit(solution)/shard_map/ppermute | solution.py:12
  84.9 7.9 %collective-permute-start.2 = (bf16[64,256]{1,0:T(8,128)(2,1)S(1)}, bf16[64,256]{1,0:T(8,128)(2,1)S(1)}, u32[]{:S(2)}, u32[]{:S(2)}) collective-permute-start(bf16[64,256]{1,0:T(8,128)(2,1)S(1)} %fusion.45), channel_id=1, source_target_pairs={{0,16},{16,0},{4,20},{20,4},{8,24},{24,8},{12,28},{28,12},{32,48},... | collective-permute-start | bytes 98312 | tf_op jit(solution)/shard_map/ppermute | solution.py:42
  92.8 8.4 %collective-permute-start.20 = (bf16[64,256]{1,0:T(8,128)(2,1)S(1)}, bf16[64,256]{1,0:T(8,128)(2,1)S(1)}, u32[]{:S(2)}, u32[]{:S(2)}) collective-permute-start(bf16[64,256]{1,0:T(8,128)(2,1)S(1)} %fusion.45), channel_id=1, source_target_pairs={{0,48},{4,52},{8,56},{12,60},{16,64},{20,68},{24,72},{28,76},{32,8... | collective-permute-start | bytes 98312 | tf_op jit(solution)/shard_map/ppermute | solution.py:12
  101.2 11.5 %collective-permute-start.19 = (bf16[64,256]{1,0:T(8,128)(2,1)S(1)}, bf16[64,256]{1,0:T(8,128)(2,1)S(1)}, u32[]{:S(2)}, u32[]{:S(2)}) collective-permute-start(bf16[64,256]{1,0:T(8,128)(2,1)S(1)} %fusion.45), channel_id=1, source_target_pairs={{48,0},{52,4},{56,8},{60,12},{64,16},{68,20},{72,24},{76,28},{80,3... | collective-permute-start | bytes 98312 | tf_op jit(solution)/shard_map/ppermute | solution.py:12
  112.7 7.4 %collective-permute-start.18 = (bf16[64,256]{1,0:T(8,128)(2,1)S(1)}, bf16[64,256]{1,0:T(8,128)(2,1)S(1)}, u32[]{:S(2)}, u32[]{:S(2)}) collective-permute-start(bf16[64,256]{1,0:T(8,128)(2,1)S(1)} %fusion.45), channel_id=1, source_target_pairs={{0,32},{4,36},{8,40},{12,44},{16,48},{20,52},{24,56},{28,60},{32,6... | collective-permute-start | bytes 98312 | tf_op jit(solution)/shard_map/ppermute | solution.py:12
  120.0 122.4 %collective-permute-start.17 = (bf16[64,256]{1,0:T(8,128)(2,1)S(1)}, bf16[64,256]{1,0:T(8,128)(2,1)}, u32[]{:S(2)}, u32[]{:S(2)}) collective-permute-start(bf16[64,256]{1,0:T(8,128)(2,1)S(1)} %fusion.45), channel_id=1, source_target_pairs={{32,0},{36,4},{40,8},{44,12},{48,16},{52,20},{56,24},{60,28},{64,3... | collective-permute-start | bytes 98312 | tf_op jit(solution)/shard_map/ppermute | solution.py:12
  121.7 19.9 %collective-permute-start.16 = (bf16[64,256]{1,0:T(8,128)(2,1)S(1)}, bf16[64,256]{1,0:T(8,128)(2,1)S(1)}, u32[]{:S(2)}, u32[]{:S(2)}) collective-permute-start(bf16[64,256]{1,0:T(8,128)(2,1)S(1)} %fusion.46), channel_id=1, source_target_pairs={{0,96},{4,100},{8,104},{12,108},{16,112},{20,116},{24,120},{28,124... | collective-permute-start | bytes 98312 | tf_op jit(solution)/shard_map/ppermute | solution.py:12
  132.5 7.5 %collective-permute-start.3 = (bf16[64,256]{1,0:T(8,128)(2,1)S(1)}, bf16[64,256]{1,0:T(8,128)(2,1)S(1)}, u32[]{:S(2)}, u32[]{:S(2)}) collective-permute-start(bf16[64,256]{1,0:T(8,128)(2,1)S(1)} %fusion.46), channel_id=1, source_target_pairs={{0,32},{32,0},{4,36},{36,4},{8,40},{40,8},{12,44},{44,12},{16,48},... | collective-permute-start | bytes 98312 | tf_op jit(solution)/shard_map/ppermute | solution.py:42
  140.0 7.6 %collective-permute-start.15 = (bf16[64,256]{1,0:T(8,128)(2,1)S(1)}, bf16[64,256]{1,0:T(8,128)(2,1)S(1)}, u32[]{:S(2)}, u32[]{:S(2)}) collective-permute-start(bf16[64,256]{1,0:T(8,128)(2,1)S(1)} %fusion.46), channel_id=1, source_target_pairs={{96,0},{100,4},{104,8},{108,12},{112,16},{116,20},{120,24},{124,28... | collective-permute-start | bytes 98312 | tf_op jit(solution)/shard_map/ppermute | solution.py:12
  141.6 7.5 %collective-permute-start.14 = (bf16[64,256]{1,0:T(8,128)(2,1)S(1)}, bf16[64,256]{1,0:T(8,128)(2,1)S(1)}, u32[]{:S(2)}, u32[]{:S(2)}) collective-permute-start(bf16[64,256]{1,0:T(8,128)(2,1)S(1)} %fusion.46), channel_id=1, source_target_pairs={{0,64},{4,68},{8,72},{12,76},{16,80},{20,84},{24,88},{28,92},{32,9... | collective-permute-start | bytes 98312 | tf_op jit(solution)/shard_map/ppermute | solution.py:12
  147.6 93.8 %collective-permute-start.13 = (bf16[64,256]{1,0:T(8,128)(2,1)S(1)}, bf16[64,256]{1,0:T(8,128)(2,1)}, u32[]{:S(2)}, u32[]{:S(2)}) collective-permute-start(bf16[64,256]{1,0:T(8,128)(2,1)S(1)} %fusion.46), channel_id=1, source_target_pairs={{64,0},{68,4},{72,8},{76,12},{80,16},{84,20},{88,24},{92,28},{96,3... | collective-permute-start | bytes 98312 | tf_op jit(solution)/shard_map/ppermute | solution.py:12
  149.0 10.0 %collective-permute-start.4 = (bf16[64,256]{1,0:T(8,128)(2,1)S(1)}, bf16[64,256]{1,0:T(8,128)(2,1)S(1)}, u32[]{:S(2)}, u32[]{:S(2)}) collective-permute-start(bf16[64,256]{1,0:T(8,128)(2,1)S(1)} %fusion.47), channel_id=1, source_target_pairs={{0,64},{64,0},{4,68},{68,4},{8,72},{72,8},{12,76},{76,12},{16,80},... | collective-permute-start | bytes 98312 | tf_op jit(solution)/shard_map/ppermute | solution.py:42
  159.0 12.1 %collective-permute-start.12 = (bf16[64,256]{1,0:T(8,128)(2,1)S(1)}, bf16[64,256]{1,0:T(8,128)(2,1)S(1)}, u32[]{:S(2)}, u32[]{:S(2)}) collective-permute-start(bf16[64,256]{1,0:T(8,128)(2,1)S(1)} %fusion.47), channel_id=1, source_target_pairs={{0,192},{4,196},{8,200},{12,204},{16,208},{20,212},{24,216},{28,22... | collective-permute-start | bytes 98312 | tf_op jit(solution)/shard_map/ppermute | solution.py:12
  171.1 11.8 %collective-permute-start.11 = (bf16[64,256]{1,0:T(8,128)(2,1)S(1)}, bf16[64,256]{1,0:T(8,128)(2,1)S(1)}, u32[]{:S(2)}, u32[]{:S(2)}) collective-permute-start(bf16[64,256]{1,0:T(8,128)(2,1)S(1)} %fusion.47), channel_id=1, source_target_pairs={{192,0},{196,4},{200,8},{204,12},{208,16},{212,20},{216,24},{220,2... | collective-permute-start | bytes 98312 | tf_op jit(solution)/shard_map/ppermute | solution.py:12
  182.9 6.8 %collective-permute-start.10 = (bf16[64,256]{1,0:T(8,128)(2,1)S(1)}, bf16[64,256]{1,0:T(8,128)(2,1)S(1)}, u32[]{:S(2)}, u32[]{:S(2)}) collective-permute-start(bf16[64,256]{1,0:T(8,128)(2,1)S(1)} %fusion.47), channel_id=1, source_target_pairs={{0,128},{4,132},{8,136},{12,140},{16,144},{20,148},{24,152},{28,15... | collective-permute-start | bytes 98312 | tf_op jit(solution)/shard_map/ppermute | solution.py:12
  189.7 13.5 %collective-permute-start.8 = (bf16[64,256]{1,0:T(8,128)(2,1)S(1)}, bf16[64,256]{1,0:T(8,128)(2,1)S(1)}, u32[]{:S(2)}, u32[]{:S(2)}) collective-permute-start(bf16[64,256]{1,0:T(8,128)(2,1)S(1)} %fusion.48), channel_id=1, source_target_pairs={{0,384},{4,388},{8,392},{12,396},{16,400},{20,404},{24,408},{28,41... | collective-permute-start | bytes 98312 | tf_op jit(solution)/shard_map/ppermute | solution.py:12
  203.3 9.7 %collective-permute-start.7 = (bf16[64,256]{1,0:T(8,128)(2,1)S(1)}, bf16[64,256]{1,0:T(8,128)(2,1)S(1)}, u32[]{:S(2)}, u32[]{:S(2)}) collective-permute-start(bf16[64,256]{1,0:T(8,128)(2,1)S(1)} %fusion.48), channel_id=1, source_target_pairs={{384,0},{388,4},{392,8},{396,12},{400,16},{404,20},{408,24},{412,2... | collective-permute-start | bytes 98312 | tf_op jit(solution)/shard_map/ppermute | solution.py:12
  213.0 2.9 %collective-permute-start.6 = (bf16[64,256]{1,0:T(8,128)(2,1)S(1)}, bf16[64,256]{1,0:T(8,128)(2,1)S(1)}, u32[]{:S(2)}, u32[]{:S(2)}) collective-permute-start(bf16[64,256]{1,0:T(8,128)(2,1)S(1)} %fusion.48), channel_id=1, source_target_pairs={{0,256},{4,260},{8,264},{12,268},{16,272},{20,276},{24,280},{28,28... | collective-permute-start | bytes 98312 | tf_op jit(solution)/shard_map/ppermute | solution.py:12
  215.9 14.5 %collective-permute-start.5 = (bf16[64,256]{1,0:T(8,128)(2,1)S(1)}, bf16[64,256]{1,0:T(8,128)(2,1)S(1)}, u32[]{:S(2)}, u32[]{:S(2)}) collective-permute-start(bf16[64,256]{1,0:T(8,128)(2,1)S(1)} %fusion.48), channel_id=1, source_target_pairs={{256,0},{260,4},{264,8},{268,12},{272,16},{276,20},{280,24},{284,2... | collective-permute-start | bytes 98312 | tf_op jit(solution)/shard_map/ppermute | solution.py:12
  230.4 1.3 copy-start.5
  230.4 10.0 %collective-permute-start.9 = (bf16[64,256]{1,0:T(8,128)(2,1)S(1)}, bf16[64,256]{1,0:T(8,128)(2,1)}, u32[]{:S(2)}, u32[]{:S(2)}) collective-permute-start(bf16[64,256]{1,0:T(8,128)(2,1)S(1)} %fusion.47), channel_id=1, source_target_pairs={{128,0},{132,4},{136,8},{140,12},{144,16},{148,20},{152,24},{156,2... | collective-permute-start | bytes 98312 | tf_op jit(solution)/shard_map/ppermute | solution.py:12
  259.6 2.7 copy-start.3
Sparse Core Ops, SparseCore 0:
  140.1 44.6 all-gather.2
where the time goes:
time: 278 us; the launch traced here: 277 us
  starting transfers between devices  118 us (42%)
  waiting for transfers between devices  69.9 us (25%)
  between operations  31.4 us (11%)
  blocking collectives  27.6 us (10%)
  matrix products  18.7 us (7%)
  local copies, waits for them, and re-layouts  5.31 us (2%)
  other arithmetic  4.5 us (2%)
    ppermute x24, starting transfers between devices, shifted(): lax.ppermute(value, axis, [(source, source + steps) for source in range(l...  90.3 us
    ppermute x24, waiting for transfers between devices, shifted(): lax.ppermute(value, axis, [(source, source + steps) for source in range(l...  62.3 us
    ppermute x5, starting transfers between devices, swapped(): return lax.ppermute(block, axis, route)  24.2 us
    all_gather x1, blocking collectives, per_device(): lax.all_gather(leaf_coef[None], 'level', axis=0, tiled=True)  15.7 us
    all_gather x1, blocking collectives, per_device(): fields = lax.all_gather(fields, 'level', axis=0, tiled=True)  12 us
    dot_general x19, matrix products, down_one(): lax.dot_general(fields, matrix, (((1,), (1,)), ((), ())), preferred_eleme...  7.76 us
    ppermute x5, waiting for transfers between devices, swapped(): return lax.ppermute(block, axis, route)  7.52 us
  transfers between devices with their start and end apart: 32, of which 16 were waited for; matrix products, arithmetic and copies ran while one was open for 6% of the time, Pallas kernels for 0%

commit v1 on v0

v1 whole, which is shorter than its diff:
```python
import functools

import jax
import jax.numpy as jnp
from jax import lax
from jax.experimental import pallas as pl
from jax.experimental.pallas import tpu as pltpu
from jax.sharding import PartitionSpec as P

MESH = pl.DeviceIdType.MESH
F32, BF16 = jnp.float32, jnp.bfloat16

PLANE = 8
MEMBERS = 4
PEERS = PLANE * MEMBERS
DEPTH = 16
ROWS = 8


def reversed_bits(value, bits):
    out = 0
    for bit in range(bits):
        out = out + ((value // (1 << bit)) % 2) * (1 << (bits - 1 - bit))
    return out


def flat(blocks):
    wide = blocks.astype(F32)
    return wide.reshape(wide.shape[0] * wide.shape[1], wide.shape[2])


def mul(rows, matrix):
    return jnp.dot(rows.astype(BF16), matrix, preferred_element_type=F32)


def mul_t(rows, matrix):
    return lax.dot_general(
        rows.astype(BF16), matrix, (((1,), (1,)), ((), ())), preferred_element_type=F32
    )


def rounded(rows):
    return rows.astype(BF16).astype(F32)


def kernel(
    x_hbm, basis_hbm, tiles_hbm, transfer_hbm, coupling_hbm, cols_ref, count_ref, mask_ref,
    out_ref,
    win, basis, tiles, trans, coup, cbuf, abuf, tree, near_z, quad_z, planes, lev4, lev5, fbuf, gbuf, acc,
    load_sem, a_send, a_recv, z_send, z_recv, d_send, d_recv, n_send, n_recv,
):
    g = lax.axis_index("leaf")
    x = lax.axis_index("level")
    z = g // PLANE
    gp = g % PLANE
    core = g % 2
    base_g = g - gp
    me = gp * MEMBERS + x
    partner_g = g + 1 - 2 * core
    beyond_g = (g + 2 * core - 1 + PLANE * DEPTH) % (PLANE * DEPTH)
    x_up, x_down = (x + 1) % MEMBERS, (x + 3) % MEMBERS

    def load(k, src, dst):
        return pltpu.make_async_copy(src, dst, load_sem.at[k])

    loads = [
        load(0, x_hbm, win.at[4 + x]),
        load(1, basis_hbm, basis),
        load(2, transfer_hbm, trans),
        load(3, tiles_hbm, tiles),
        load(4, coupling_hbm, coup),
    ]
    for item in loads:
        item.start()

    barrier = pltpu.get_barrier_semaphore()

    def greet(j, carry):
        other = (me + j) % PEERS
        pl.semaphore_signal(
            barrier, inc=1, device_id=(base_g + other // MEMBERS, other % MEMBERS), device_id_type=MESH
        )
        return carry

    lax.fori_loop(1, PEERS, greet, 0)

    def greet_z(j, carry):
        pl.semaphore_signal(
            barrier, inc=1, device_id=(((z + j) % DEPTH) * PLANE + gp, x), device_id_type=MESH
        )
        return carry

    lax.fori_loop(1, DEPTH, greet_z, 0)
    pl.semaphore_signal(barrier, inc=1, device_id=(beyond_g, x), device_id_type=MESH)

    loads[0].wait()
    loads[1].wait()
    coef = jnp.dot(win[4 + x], basis[0], preferred_element_type=F32)
    cbuf[...] = coef.reshape(PEERS, ROWS, coef.shape[1]).astype(BF16)

    pl.semaphore_wait(barrier, PEERS - 1 + DEPTH - 1 + 1)

    my_slot = reversed_bits(me, 5)

    def send_a(j, carry):
        other = (me + j) % PEERS
        pltpu.make_async_remote_copy(
            src_ref=cbuf.at[other],
            dst_ref=abuf.at[my_slot],
            send_sem=a_send,
            recv_sem=a_recv,
            device_id=(base_g + other // MEMBERS, other % MEMBERS),
            device_id_type=MESH,
        ).start()
        return carry

    lax.fori_loop(1, PEERS, send_a, 0)
    pltpu.make_async_copy(cbuf.at[me], abuf.at[my_slot], a_recv).start()

    own = win.at[4 + x]

    def near_copy(src, dst, where, k):
        return pltpu.make_async_remote_copy(
            src_ref=src, dst_ref=dst, send_sem=n_send, recv_sem=n_recv.at[k],
            device_id=where, device_id_type=MESH,
        )

    near_copy(own, win.at[4 + x], (g, x_up), 0).start()
    near_copy(own, win.at[4 + x], (g, x_down), 1).start()

    def pass_on(member):
        near_copy(win.at[4 + member], win.at[8 * (1 - core) + member], (beyond_g, x), 4).start()
        near_copy(win.at[4 + member], win.at[8 * core + member], (partner_g, x), 5).start()

    pass_on(x)

    def arrived(ref, sem):
        pltpu.make_async_copy(ref, ref, sem).wait()

    loads[3].wait()
    acc[...] = jnp.dot(win[4 + x], tiles[0, 0], preferred_element_type=F32)
    loads[2].wait()
    loads[4].wait()

    arrived(abuf, a_recv)
    rows = flat(abuf[...])
    steps = []
    for _ in range(5):
        half = rows.shape[0] // 2
        rows = rounded(mul(rows[:half], trans[0]) + mul(rows[half:], trans[1]))
        steps.append(rows)
    at = 0
    for part in steps[1:]:
        blocks = part.shape[0] // ROWS
        tree[at : at + blocks] = part.reshape(blocks, ROWS, part.shape[1]).astype(BF16)
        at += blocks

    def send_plane(j, carry):
        pltpu.make_async_remote_copy(
            src_ref=tree.at[14], dst_ref=planes.at[z], send_sem=z_send.at[0], recv_sem=z_recv.at[0],
            device_id=(((z + j) % DEPTH) * PLANE + gp, x), device_id_type=MESH,
        ).start()
        return carry

    lax.fori_loop(1, DEPTH, send_plane, 0)
    pltpu.make_async_copy(tree.at[14], planes.at[z], z_recv.at[0]).start()
    for side, step in ((0, 1), (1, DEPTH - 1)):
        pltpu.make_async_remote_copy(
            src_ref=tree.at[0:14], dst_ref=near_z.at[side], send_sem=z_send.at[1 + side],
            recv_sem=z_recv.at[1 + side],
            device_id=(((z + step) % DEPTH) * PLANE + gp, x), device_id_type=MESH,
        ).start()
    for side, step in ((0, 2), (1, DEPTH - 2)):
        pltpu.make_async_remote_copy(
            src_ref=tree.at[12:14], dst_ref=quad_z.at[side], send_sem=z_send.at[3 + side],
            recv_sem=z_recv.at[3 + side],
            device_id=(((z + step) % DEPTH) * PLANE + gp, x), device_id_type=MESH,
        ).start()

    half_rows = win.shape[1] // 2
    arrived(win.at[4 + x_down], n_recv.at[0])
    arrived(win.at[4 + x_up], n_recv.at[1])
    near_copy(
        win.at[4 + x_down, 0:half_rows], win.at[4 + x_down, 0:half_rows], (g, x_up), 2
    ).start()
    near_copy(
        win.at[4 + x_up, half_rows : 2 * half_rows], win.at[4 + x_up, half_rows : 2 * half_rows], (g, x_down), 3
    ).start()
    pass_on(x_down)
    pass_on(x_up)

    def flag(level, pick, index, valid):
        return mask_ref[level, pick, index].astype(F32) * jnp.where(valid, 1.0, 0.0)

    def couple(level, sources):
        total = 0.0
        for pick in range(2):
            ahead, behind = sources(pick)
            total = total + mul(ahead, coup[level, pick]) + mul_t(behind, coup[level, pick])
        return total

    inside_low, inside_high = z > 0, z < DEPTH - 1

    def low_level(level, blocks, start, bits, far_low, far_high):
        def fetch(place):
            if 0 <= place < blocks:
                return tree[start + reversed_bits(place, bits)], True
            if -blocks <= place < 0:
                return near_z[0, start + reversed_bits(place + blocks, bits)], z >= 1
            if blocks <= place < 2 * blocks:
                return near_z[1, start + reversed_bits(place - blocks, bits)], z < DEPTH - 1
            if place < -blocks:
                return far_low(place + 2 * blocks), z >= 2
            return far_high(place - 2 * blocks), z < DEPTH - 2

        def sources(pick):
            offset = pick + 2
            ahead, behind = [], []
            for slot in range(blocks):
                place = reversed_bits(slot, bits)
                block, valid = fetch(place + offset)
                ahead.append(block.astype(F32) * flag(level, pick, z * blocks + place, valid))
                block, valid = fetch(place - offset)
                index = (z * blocks + place - offset + DEPTH * blocks) % (DEPTH * blocks)
                behind.append(block.astype(F32) * flag(level, pick, index, valid))
            return jnp.concatenate(ahead, axis=0), jnp.concatenate(behind, axis=0)

        return couple(level, sources)

    for side in range(2):
        arrived(near_z.at[side], z_recv.at[1 + side])
        arrived(quad_z.at[side], z_recv.at[3 + side])
    coupled0 = low_level(0, 8, 0, 3, None, None)
    coupled1 = low_level(1, 4, 8, 2, None, None)
    coupled2 = low_level(2, 2, 12, 1, lambda q: quad_z[0, q], lambda q: quad_z[1, q])

    arrived(win.at[4 + (x + 2) % MEMBERS, 0:half_rows], n_recv.at[2])
    arrived(win.at[4 + (x + 2) % MEMBERS, half_rows : 2 * half_rows], n_recv.at[3])
    pass_on((x + 2) % MEMBERS)

    arrived(planes, z_recv.at[0])

    def join(ref, count):
        lower = jnp.concatenate([ref[2 * k].astype(F32) for k in range(count)], axis=0)
        upper = jnp.concatenate([ref[2 * k + 1].astype(F32) for k in range(count)], axis=0)
        return rounded(mul(lower, trans[0]) + mul(upper, trans[1]))

    lev4[...] = join(planes, 8).reshape(lev4.shape)
    lev5[...] = join(lev4, 4).reshape(lev5.shape)

    def high_level(level, ref, count, here):
        def sources(pick):
            offset = pick + 2
            ahead = ref[(here + offset) % count].astype(F32) * flag(level, pick, here, here + offset < count)
            index = (here + count - offset) % count
            behind = ref[index].astype(F32) * flag(level, pick, index, here >= offset)
            return ahead, behind

        return couple(level, sources)

    coupled3 = high_level(3, planes, DEPTH, z)
    coupled4 = high_level(4, lev4, DEPTH // 2, z // 2)
    coupled5 = high_level(5, lev5, DEPTH // 4, z // 4)

    field = mul_t(coupled5, trans[(z // 2) % 2]) + coupled4
    field = mul_t(field, trans[z % 2]) + coupled3
    for coupled in (coupled2, coupled1, coupled0):
        field = jnp.concatenate([mul_t(field, trans[0]), mul_t(field, trans[1])], axis=0) + coupled
    fbuf[...] = field.reshape(fbuf.shape).astype(BF16)

    def send_d(j, carry):
        other = (me + j) % PEERS
        pltpu.make_async_remote_copy(
            src_ref=fbuf.at[reversed_bits(other // MEMBERS, 3)],
            dst_ref=gbuf.at[me],
            send_sem=d_send,
            recv_sem=d_recv,
            device_id=(base_g + other // MEMBERS, other % MEMBERS),
            device_id_type=MESH,
        ).start()
        return carry

    lax.fori_loop(1, PEERS, send_d, 0)
    pltpu.make_async_copy(fbuf.at[reversed_bits(gp, 3)], gbuf.at[me], d_recv).start()

    arrived(win.at[pl.ds(8 * core, 4)], n_recv.at[4])
    arrived(win.at[pl.ds(8 * (1 - core), 4)], n_recv.at[5])
    live = count_ref[0]
    leaf_low = (g - 1) * MEMBERS

    def weight(slot, col):
        leaf = leaf_low + col
        good = (leaf >= 0) & (leaf < PLANE * DEPTH * MEMBERS) & (slot < live)
        return jnp.where(good, 1.0, 0.0)

    slot_cols = (4 + x, 3 + x, 5 + x, cols_ref[0, 3])
    for slot in range(1, 4):
        col = slot_cols[slot]
        product = jnp.dot(win[col], tiles[0, slot], preferred_element_type=F32)
        acc[...] = acc[...] + weight(slot, col) * product

    arrived(gbuf, d_recv)
    field = flat(gbuf[...])
    field = mul_t(field, trans[x // 2])
    field = mul_t(field, trans[x % 2])
    out_ref[...] = (acc[...] + mul_t(field, basis[0])).astype(out_ref.dtype)

    arrived(cbuf.at[0 : PEERS - 1], a_send)
    arrived(gbuf.at[0 : PEERS - 1], d_send)
    arrived(planes.at[0 : DEPTH - 1], z_send.at[0])
    for side in range(2):
        arrived(near_z.at[side], z_send.at[1 + side])
        arrived(quad_z.at[side], z_send.at[3 + side])
    arrived(win.at[0:11], n_send)


def per_device(points_x, leaf_basis, near_tiles, near_cols, near_count, transfer, coupling, couple_mask):
    vectors, points = points_x.shape
    rank = leaf_basis.shape[2]
    hbm = pl.BlockSpec(memory_space=pl.ANY)
    smem = pl.BlockSpec(memory_space=pltpu.SMEM)
    block = (ROWS, rank)
    dma = pltpu.SemaphoreType.DMA
    return pl.pallas_call(
        kernel,
        out_shape=jax.ShapeDtypeStruct((vectors, points), BF16),
        in_specs=[hbm] * 5 + [smem] * 3,
        out_specs=pl.BlockSpec(memory_space=pltpu.VMEM),
        scratch_shapes=[
            pltpu.VMEM((12, vectors, points), BF16),
            pltpu.VMEM(leaf_basis.shape, BF16),
            pltpu.VMEM(near_tiles.shape, BF16),
            pltpu.VMEM(transfer.shape, BF16),
            pltpu.VMEM(coupling.shape, BF16),
            pltpu.VMEM((PEERS,) + block, BF16),
            pltpu.VMEM((PEERS,) + block, BF16),
            pltpu.VMEM((16,) + block, BF16),
            pltpu.VMEM((2, 14) + block, BF16),
            pltpu.VMEM((2, 2) + block, BF16),
            pltpu.VMEM((DEPTH,) + block, BF16),
            pltpu.VMEM((DEPTH // 2,) + block, F32),
            pltpu.VMEM((DEPTH // 4,) + block, F32),
            pltpu.VMEM((PLANE,) + block, BF16),
            pltpu.VMEM((PEERS,) + block, BF16),
            pltpu.VMEM((vectors, points), F32),
            dma((5,)), dma(()), dma(()), dma((5,)), dma((5,)), dma(()), dma(()), dma(()), dma((6,)),
        ],
        compiler_params=pltpu.CompilerParams(
            collective_id=0, has_side_effects=True, vmem_limit_bytes=48 * 1024 * 1024
        ),
    )(
        points_x, leaf_basis, near_tiles, transfer, coupling,
        near_cols, near_count, jnp.transpose(couple_mask, (0, 2, 1)),
    )


def solution(mesh):
    in_specs = (
        P(None, ("leaf", "level")),
        P(("leaf", "level"), None, None),
        P(("leaf", "level"), None, None, None),
        P(("leaf", "level"), None),
        P(("leaf", "level")),
        P(),
        P(),
        P(),
    )
    out_specs = P(None, ("leaf", "level"))
    return jax.shard_map(per_device, mesh=mesh, in_specs=in_specs, out_specs=out_specs, check_vma=False)
```

time: 278 us -> 52.3 us (0.19)
  the two profiles are of different devices: /device:TPU:2 before, /device:TPU:1 now
where the time goes in v1:
time: 52.3 us; the launch traced here: 52 us
  Pallas kernels  43.4 us (83%)
  local copies, waits for them, and re-layouts  7.89 us (15%)
  between operations  0.67 us (1%)
    pallas_call x1, Pallas kernels, per_device(): pl.pallas_call(kernel, out_shape=jax.ShapeDtypeStruct((vectors, points),...  43.4 us
    unnamed x15, local copies, waits for them, and re-layouts  7.89 us

profile of v1, /device:TPU:1, one launch (start us, length us, event | category | flops | bytes accessed | tf_op | source)
XLA Modules:
  0.0 52.0 jit_solution(1329280125217760516)
XLA Ops:
  0.7 0.0 copy-start
  0.7 1.6 %copy-done = bf16[1,4,512,512]{3,2,1,0:T(8,128)(2,1)S(1)} copy-done((bf16[1,4,512,512]{3,2,1,0:T(8,128)(2,1)S(1)}, bf16[1,4,512,512]{3,2,1,0:T(8,128)(2,1)}, u32[]{:S(2)}) %copy-start) | copy-done | bytes 2097176
  2.2 0.0 copy-start.1
  2.2 1.4 %copy-done.1 = bf16[6,2,256,256]{3,2,1,0:T(8,128)(2,1)S(1)} copy-done((bf16[6,2,256,256]{3,2,1,0:T(8,128)(2,1)S(1)}, bf16[6,2,256,256]{3,2,1,0:T(8,128)(2,1)}, u32[]{:S(2)}) %copy-start.1) | copy-done | bytes 1572888
  3.7 0.0 copy-start.2
  3.7 0.9 %copy-done.2 = bf16[256,512]{1,0:T(8,128)(2,1)S(1)} copy-done((bf16[256,512]{1,0:T(8,128)(2,1)S(1)}, bf16[256,512]{1,0:T(8,128)(2,1)}, u32[]{:S(2)}) %copy-start.2) | copy-done | bytes 262168
  4.6 0.0 copy-start.3
  4.6 0.9 %copy-done.3 = bf16[1,512,256]{2,1,0:T(8,128)(2,1)S(1)} copy-done((bf16[1,512,256]{2,1,0:T(8,128)(2,1)S(1)}, bf16[1,512,256]{2,1,0:T(8,128)(2,1)}, u32[]{:S(2)}) %copy-start.3) | copy-done | bytes 262168
  5.6 0.0 copy-start.4
  5.6 0.9 %copy-done.4 = bf16[2,256,256]{2,1,0:T(8,128)(2,1)S(1)} copy-done((bf16[2,256,256]{2,1,0:T(8,128)(2,1)S(1)}, bf16[2,256,256]{2,1,0:T(8,128)(2,1)}, u32[]{:S(2)}) %copy-start.4) | copy-done | bytes 262168
  6.5 0.0 copy-start.5
  6.5 0.7 %copy-done.5 = s32[6,128,2]{1,2,0:T(2,128)S(1)} copy-done((s32[6,128,2]{1,2,0:T(2,128)S(1)}, s32[6,128,2]{1,2,0:T(2,128)}, u32[]{:S(2)}) %copy-start.5) | copy-done | bytes 6168
  7.2 0.0 copy-start.6
  7.2 0.7 %copy-done.6 = s32[1,4]{1,0:T(1,128)S(1)} copy-done((s32[1,4]{1,0:T(1,128)S(1)}, s32[1,4]{1,0:T(1,128)}, u32[]{:S(2)}) %copy-start.6) | copy-done | bytes 40
  7.9 43.4 %shard_map.82 = bf16[256,512]{1,0:T(8,128)(2,1)S(1)} custom-call(bf16[256,512]{1,0:T(8,128)(2,1)S(1)} %copy-done.2, bf16[1,512,256]{2,1,0:T(8,128)(2,1)S(1)} %copy-done.3, bf16[1,4,512,512]{3,2,1,0:T(8,128)(2,1)S(1)} %copy-done, bf16[2,256,256]{2,1,0:T(8,128)(2,1)S(1)} %copy-done.4, bf16[6,2,256,256]{3,2,1,0:T(8,128)(2,1)S(1)} %copy-done.1, ...), custom_call_target="tpu_custom_call" | custom-call | tf_op jit(solution)/shard_map/pallas_call | solution.py:324
  51.3 0.7 %copy.11 = bf16[256,512]{1,0:T(8,128)(2,1)} copy(bf16[256,512]{1,0:T(8,128)(2,1)S(1)} %shard_map.82) | data formatting | bytes 524288
Async XLA Ops:
  0.7 1.6 %copy-start = (bf16[1,4,512,512]{3,2,1,0:T(8,128)(2,1)S(1)}, bf16[1,4,512,512]{3,2,1,0:T(8,128)(2,1)}, u32[]{:S(2)}) copy-start(bf16[1,4,512,512]{3,2,1,0:T(8,128)(2,1)} %tiles_hbm.1) | copy-start | bytes 6291460
  2.2 1.4 %copy-start.1 = (bf16[6,2,256,256]{3,2,1,0:T(8,128)(2,1)S(1)}, bf16[6,2,256,256]{3,2,1,0:T(8,128)(2,1)}, u32[]{:S(2)}) copy-start(bf16[6,2,256,256]{3,2,1,0:T(8,128)(2,1)} %coupling_hbm.1) | copy-start | bytes 4718596
  3.7 0.9 %copy-start.2 = (bf16[256,512]{1,0:T(8,128)(2,1)S(1)}, bf16[256,512]{1,0:T(8,128)(2,1)}, u32[]{:S(2)}) copy-start(bf16[256,512]{1,0:T(8,128)(2,1)} %x_hbm.1) | copy-start | bytes 786436
  4.6 0.9 %copy-start.3 = (bf16[1,512,256]{2,1,0:T(8,128)(2,1)S(1)}, bf16[1,512,256]{2,1,0:T(8,128)(2,1)}, u32[]{:S(2)}) copy-start(bf16[1,512,256]{2,1,0:T(8,128)(2,1)} %basis_hbm.1) | copy-start | bytes 786436
  5.6 0.9 %copy-start.4 = (bf16[2,256,256]{2,1,0:T(8,128)(2,1)S(1)}, bf16[2,256,256]{2,1,0:T(8,128)(2,1)}, u32[]{:S(2)}) copy-start(bf16[2,256,256]{2,1,0:T(8,128)(2,1)} %transfer_hbm.1) | copy-start | bytes 786436
  6.5 0.7 %copy-start.5 = (s32[6,128,2]{1,2,0:T(2,128)S(1)}, s32[6,128,2]{1,2,0:T(2,128)}, u32[]{:S(2)}) copy-start(s32[6,128,2]{1,2,0:T(2,128)} %param.15) | copy-start | bytes 18436
  7.2 0.7 %copy-start.6 = (s32[1,4]{1,0:T(1,128)S(1)}, s32[1,4]{1,0:T(1,128)}, u32[]{:S(2)}) copy-start(s32[1,4]{1,0:T(1,128)} %cols_ref.1) | copy-start | bytes 52

commit v2 on v1

v2 whole, which is shorter than its diff:
```python
import jax
import jax.numpy as jnp
from jax import lax
from jax.experimental import pallas as pl
from jax.experimental.pallas import tpu as pltpu
from jax.sharding import PartitionSpec as P

MESH = pl.DeviceIdType.MESH
F32, BF16 = jnp.float32, jnp.bfloat16

PLANE = 8
MEMBERS = 4
PEERS = PLANE * MEMBERS
DEPTH = 16
GROUPS = PLANE * DEPTH
ROWS = 8
EARLY = 6
SEL, EDGE = 8, 9

REACH = (0, 1, 2, 1)
PEER_STEPS = sorted(
    ((dx, dy, dc) for dx in range(4) for dy in range(4) for dc in range(2) if (dx, dy, dc) != (0, 0, 0)),
    key=lambda s: -(REACH[s[0]] + REACH[s[1]]),
)
DEPTH_STEPS = sorted(range(1, DEPTH), key=lambda s: -min(s, DEPTH - s))


def flat(blocks):
    wide = blocks.astype(F32)
    return wide.reshape(wide.shape[0] * wide.shape[1], wide.shape[2])


def mul(rows, matrix):
    return jnp.dot(rows.astype(BF16), matrix, preferred_element_type=F32)


def mul_t(rows, matrix):
    return lax.dot_general(
        rows.astype(BF16), matrix, (((1,), (1,)), ((), ())), preferred_element_type=F32
    )


def rounded(rows):
    return rows.astype(BF16).astype(F32)


def piece(rows, index):
    return rows[ROWS * index : ROWS * (index + 1)]


def kernel(
    count_ref, x_hbm, basis_hbm, tiles_hbm, transfer_hbm, coupling_hbm, cols_hbm, mask_hbm,
    out_ref,
    win, basis, tiles, trans, coup, mask_ref, cols_ref,
    cbuf, abuf, tree, near_z, quad_z, planes, fbuf, gbuf, acc, low,
    two, three, ahead_mats, behind_mats, ask, asked, chosen,
    load_sem, a_send, a_recv, z_send, z_recv, d_send, d_recv, n_send, n_recv, above_sem,
):
    g = lax.axis_index("leaf")
    x = lax.axis_index("level")
    z = g // PLANE
    gp = g % PLANE
    core = g % 2
    y = gp // 2
    base_g = g - gp
    me = gp * MEMBERS + x
    rank = trans.shape[2]
    partner_g = g + 1 - 2 * core
    beyond_g = (g + 2 * core - 1 + GROUPS) % GROUPS
    has_beyond = (g > 0) & (g < GROUPS - 1)
    at_edge = x == core * (MEMBERS - 1)
    x_up, x_down, x_far = (x + 1) % MEMBERS, (x + 3) % MEMBERS, (x + 2) % MEMBERS

    def load(k, src, dst):
        return pltpu.make_async_copy(src, dst, load_sem.at[k])

    load_x = load(0, x_hbm, win.at[x])
    load_basis = load(1, basis_hbm, basis)
    load_trans = load(2, transfer_hbm, trans)
    load_cols = load(3, cols_hbm, cols_ref)
    load_mask = load(4, mask_hbm, mask_ref)
    load_coup = load(5, coupling_hbm, coup)
    load_tiles = load(6, tiles_hbm, tiles)
    for item in (load_basis, load_trans, load_x, load_cols, load_mask, load_coup, load_tiles):
        item.start()

    def plane_peer(step):
        dx, dy, dc = step
        other_core = 1 - core if dc else core
        other_y = (y + dy) % 4
        return other_y * 2 + other_core, (x + dx) % MEMBERS

    def z_peer(step):
        return ((z + step) % DEPTH) * PLANE + gp, x

    barrier = pltpu.get_barrier_semaphore()

    def greet_above(plane, carry):
        pl.semaphore_signal(barrier, inc=1, device_id=(plane * PLANE + gp, x), device_id_type=MESH)
        return carry

    lax.fori_loop(z + 1, DEPTH, greet_above, 0)
    for step in PEER_STEPS:
        other_gp, other_x = plane_peer(step)
        pl.semaphore_signal(barrier, inc=1, device_id=(base_g + other_gp, other_x), device_id_type=MESH)
    edge_x = (MEMBERS - 1) * (1 - core)

    @pl.when(has_beyond)
    def _():
        pl.semaphore_signal(barrier, inc=1, device_id=(beyond_g, x), device_id_type=MESH)

    @pl.when(has_beyond & at_edge)
    def _():
        pl.semaphore_signal(barrier, inc=1, device_id=(beyond_g, edge_x), device_id_type=MESH)

    def arrived(ref, sem):
        pltpu.make_async_copy(ref, ref, sem).wait()

    load_trans.wait()
    load_basis.wait()
    up = mul(basis[0], trans[x % 2])
    basis[0] = mul(up, trans[x // 2]).astype(BF16)
    load_x.wait()
    coef = jnp.dot(win[x], basis[0], preferred_element_type=F32)
    cbuf[...] = coef.reshape(PEERS, ROWS, rank).astype(BF16)

    @pl.when(jnp.logical_not(has_beyond))
    def _():
        win[SEL] = jnp.zeros(win.shape[1:], BF16)
        win[EDGE] = jnp.zeros(win.shape[1:], BF16)

    load_cols.wait()
    extra = cols_ref[0, 3]
    wanted = jnp.where(core == 0, extra, extra - 2 * MEMBERS)
    ask[...] = jnp.broadcast_to(wanted.astype(F32), ask.shape)

    greeted = PEERS - 1 + z + jnp.where(has_beyond, 1, 0) + jnp.where(has_beyond & at_edge, 1, 0)
    pl.semaphore_wait(barrier, greeted)

    def greet_below(plane, carry):
        pl.semaphore_signal(above_sem, inc=1, device_id=(plane * PLANE + gp, x), device_id_type=MESH)
        return carry

    lax.fori_loop(0, z, greet_below, 0)

    def near_copy(src, dst, where, send, recv):
        return pltpu.make_async_remote_copy(
            src_ref=src, dst_ref=dst, send_sem=n_send.at[send], recv_sem=n_recv.at[recv],
            device_id=where, device_id_type=MESH,
        )

    ask_copy = near_copy(ask, asked, (beyond_g, x), 3, 7)

    @pl.when(has_beyond)
    def _():
        ask_copy.start()

    half = win.shape[1] // 2

    def first(place):
        return win.at[place, 0:half]

    def last(place):
        return win.at[place, half : 2 * half]

    def share():
        near_copy(first(x), first(x), (g, x_up), 0, 0).start()
        near_copy(last(x), last(x), (g, x_down), 0, 1).start()
        near_copy(last(x), last(x), (g, x_up), 0, 8).start()
        near_copy(first(x), first(x), (g, x_down), 0, 9).start()
        near_copy(win.at[x], win.at[4 + x], (partner_g, x), 0, 4).start()

    my_slot = x * PLANE + gp
    for step in PEER_STEPS:
        other_gp, other_x = plane_peer(step)
        pltpu.make_async_remote_copy(
            src_ref=cbuf.at[other_gp * MEMBERS + other_x], dst_ref=abuf.at[my_slot],
            send_sem=a_send, recv_sem=a_recv,
            device_id=(base_g + other_gp, other_x), device_id_type=MESH,
        ).start()
    pltpu.make_async_copy(cbuf.at[me], abuf.at[my_slot], a_recv).start()

    @pl.when(z < EARLY)
    def _():
        share()

    both = trans[...].reshape(2 * rank, rank)
    for upper in range(2):
        two[2 * rank * upper : 2 * rank * (upper + 1)] = mul(both, trans[upper]).astype(BF16)
    for upper in range(2):
        three[4 * rank * upper : 4 * rank * (upper + 1)] = mul(two[...], trans[upper]).astype(BF16)

    sel_copy = near_copy(chosen, win.at[SEL], (beyond_g, x), 1, 5)
    edge_copy = near_copy(win.at[x], win.at[EDGE], (beyond_g, edge_x), 2, 6)
    sends_edge = has_beyond & at_edge
    lanes = ask.shape[1]

    def relay():
        arrived(first(x_down), n_recv.at[0])
        near_copy(first(x_down), first(x_down), (g, x_up), 0, 2).start()
        arrived(last(x_up), n_recv.at[1])
        near_copy(last(x_up), last(x_up), (g, x_down), 0, 3).start()
        arrived(last(x_down), n_recv.at[8])
        arrived(first(x_up), n_recv.at[9])
        near_copy(win.at[x_down], win.at[4 + x_down], (partner_g, x), 0, 4).start()
        near_copy(win.at[x_up], win.at[4 + x_up], (partner_g, x), 0, 4).start()

    def relay_far():
        arrived(first(x_far), n_recv.at[2])
        arrived(last(x_far), n_recv.at[3])
        near_copy(win.at[x_far], win.at[4 + x_far], (partner_g, x), 0, 4).start()

        @pl.when(has_beyond)
        def _():
            arrived(asked, n_recv.at[7])
            tile = asked[...]
            for at in range(0, win.shape[2], lanes):
                total = 0.0
                for member in range(MEMBERS):
                    part = win[member, :, at : at + lanes].astype(F32)
                    part = part.reshape(part.shape[0] // ask.shape[0], ask.shape[0], lanes)
                    total = total + part * jnp.where(tile == member, 1.0, 0.0)[None]
                chosen[:, at : at + lanes] = total.reshape(chosen.shape[0], lanes).astype(BF16)
            sel_copy.start()

        @pl.when(sends_edge)
        def _():
            edge_copy.start()

    arrived(abuf, a_recv)
    rows = flat(abuf[...])
    share_rows = PLANE * ROWS
    tops = rounded(sum(rows[share_rows * k : share_rows * (k + 1)] for k in range(MEMBERS)))
    in_line = jnp.concatenate([piece(tops, k) for k in range(PLANE)], axis=1)
    tree[14] = mul(in_line, three[...]).astype(BF16)

    @pl.when(z < EARLY)
    def _():
        relay()

    @pl.when(z < DEPTH - 1)
    def _():
        pl.semaphore_wait(above_sem, DEPTH - 1 - z)

    for step in DEPTH_STEPS:
        pltpu.make_async_remote_copy(
            src_ref=tree.at[14], dst_ref=planes.at[z], send_sem=z_send.at[0], recv_sem=z_recv.at[0],
            device_id=z_peer(step), device_id_type=MESH,
        ).start()
    pltpu.make_async_copy(tree.at[14], planes.at[z], z_recv.at[0]).start()

    def join(parts):
        count = parts.shape[0] // (2 * ROWS)
        lower = jnp.concatenate([piece(parts, 2 * k) for k in range(count)], axis=0)
        upper = jnp.concatenate([piece(parts, 2 * k + 1) for k in range(count)], axis=0)
        return rounded(mul(lower, trans[0]) + mul(upper, trans[1]))

    pairs = join(tops)
    quads = join(pairs)
    at = 0
    for part in (tops, pairs, quads):
        blocks = part.shape[0] // ROWS
        tree[at : at + blocks] = part.reshape(blocks, ROWS, rank).astype(BF16)
        at += blocks
    for side, step in ((0, 1), (1, DEPTH - 1)):
        pltpu.make_async_remote_copy(
            src_ref=tree.at[0:14], dst_ref=near_z.at[side], send_sem=z_send.at[1 + side],
            recv_sem=z_recv.at[1 + side], device_id=z_peer(step), device_id_type=MESH,
        ).start()
    for side, step in ((0, 2), (1, DEPTH - 2)):
        pltpu.make_async_remote_copy(
            src_ref=tree.at[12:14], dst_ref=quad_z.at[side], send_sem=z_send.at[3 + side],
            recv_sem=z_recv.at[3 + side], device_id=z_peer(step), device_id_type=MESH,
        ).start()

    @pl.when(z >= EARLY)
    def _():
        share()

    load_coup.wait()
    down_two = two[pl.ds(pl.multiple_of((z % 4) * rank, rank), rank), :]
    down_one = trans[z % 2]
    for pick in range(2):
        for place, level, down in ((pick, 5, down_two), (2 + pick, 4, down_one)):
            matrix = coup[level, pick]
            at = rank * place
            ahead_mats[at : at + rank, :] = mul_t(matrix, down).astype(BF16)
            behind_mats[:, at : at + rank] = mul(down, matrix).astype(BF16)
        at = rank * (4 + pick)
        ahead_mats[at : at + rank, :] = coup[3, pick]
        behind_mats[:, at : at + rank] = coup[3, pick]

    load_tiles.wait()
    acc[...] = jnp.dot(win[x], tiles[0, 0], preferred_element_type=F32)

    @pl.when(z >= EARLY)
    def _():
        relay()

    relay_far()
    load_mask.wait()

    def flag(level, pick, index, valid):
        return mask_ref[level, pick, index].astype(F32) * jnp.where(valid, 1.0, 0.0)

    def low_level(level, blocks, start):
        def fetch(place):
            if 0 <= place < blocks:
                return tree[start + place], True
            if -blocks <= place < 0:
                return near_z[0, start + place + blocks], z >= 1
            if blocks <= place < 2 * blocks:
                return near_z[1, start + place - blocks], z < DEPTH - 1
            if place < -blocks:
                return quad_z[0, place + 2 * blocks], z >= 2
            return quad_z[1, place - 2 * blocks], z < DEPTH - 2

        total = 0.0
        for pick in range(2):
            offset = pick + 2
            ahead, behind = [], []
            for place in range(blocks):
                block, valid = fetch(place + offset)
                ahead.append(block.astype(F32) * flag(level, pick, z * blocks + place, valid))
                block, valid = fetch(place - offset)
                index = (z * blocks + place - offset + DEPTH * blocks) % (DEPTH * blocks)
                behind.append(block.astype(F32) * flag(level, pick, index, valid))
            total = total + mul(jnp.concatenate(ahead, axis=0), coup[level, pick])
            total = total + mul_t(jnp.concatenate(behind, axis=0), coup[level, pick])
        return total

    def split(parents):
        lower, upper = mul_t(parents, trans[0]), mul_t(parents, trans[1])
        parts = []
        for k in range(parents.shape[0] // ROWS):
            parts += [piece(lower, k), piece(upper, k)]
        return jnp.concatenate(parts, axis=0)

    for side in range(2):
        arrived(near_z.at[side], z_recv.at[1 + side])
        arrived(quad_z.at[side], z_recv.at[3 + side])
    low[...] = split(split(low_level(2, 2, 12)) + low_level(1, 4, 8)) + low_level(0, 8, 0)

    arrived(planes, z_recv.at[0])
    pair, quad = z // 2, z // 4
    steps = (2, 3, -2, -3)

    def gathered(count, here, index):
        return jnp.concatenate(
            [planes[index((here + step + count) % count)].astype(F32) for step in steps], axis=0
        )

    level5 = sum(
        mul(gathered(4, quad, lambda k, r=r: 4 * k + r), two[rank * r : rank * (r + 1)]) for r in range(4)
    )
    level4 = sum(mul(gathered(8, pair, lambda k, r=r: 2 * k + r), trans[r]) for r in range(2))
    level3 = gathered(DEPTH, z, lambda k: k)

    def flagged(level, rows, count, here):
        ahead, behind = [], []
        for pick in range(2):
            offset = pick + 2
            ahead.append(piece(rows, pick) * flag(level, pick, here, here + offset < count))
            index = (here + count - offset) % count
            behind.append(piece(rows, 2 + pick) * flag(level, pick, index, here >= offset))
        return ahead, behind

    ahead, behind = [], []
    for level, rows, count, here in (
        (5, rounded(level5), 4, quad), (4, rounded(level4), 8, pair), (3, level3, DEPTH, z),
    ):
        one, other = flagged(level, rows, count, here)
        ahead += one
        behind += other
    field = mul(jnp.concatenate(ahead, axis=1), ahead_mats[...])
    field = field + mul_t(jnp.concatenate(behind, axis=1), behind_mats[...])
    spread = mul_t(field, three[...])
    spread = jnp.concatenate([spread[:, rank * k : rank * (k + 1)] for k in range(PLANE)], axis=0)
    fbuf[...] = (spread + low[...]).reshape(fbuf.shape).astype(BF16)

    for step in PEER_STEPS:
        other_gp, other_x = plane_peer(step)
        pltpu.make_async_remote_copy(
            src_ref=fbuf.at[other_gp], dst_ref=gbuf.at[me], send_sem=d_send, recv_sem=d_recv,
            device_id=(base_g + other_gp, other_x), device_id_type=MESH,
        ).start()
    pltpu.make_async_copy(fbuf.at[gp], gbuf.at[me], d_recv).start()

    arrived(win.at[4:8], n_recv.at[4])

    @pl.when(sends_edge)
    def _():
        arrived(win.at[EDGE], n_recv.at[6])

    before = jnp.where(x > 0, x - 1, jnp.where(core == 1, 7, EDGE))
    after = jnp.where(x < MEMBERS - 1, x + 1, jnp.where(core == 0, 4, EDGE))
    acc[...] = (
        acc[...]
        + jnp.dot(win[before], tiles[0, 1], preferred_element_type=F32)
        + jnp.dot(win[after], tiles[0, 2], preferred_element_type=F32)
    )

    @pl.when(has_beyond)
    def _():
        arrived(win.at[SEL], n_recv.at[5])

    low_col, high_col = extra < MEMBERS, extra >= 2 * MEMBERS
    if_first = jnp.where(low_col, SEL, extra - MEMBERS)
    if_second = jnp.where(high_col, SEL, jnp.where(low_col, extra + MEMBERS, extra - MEMBERS))
    place = jnp.where(core == 0, if_first, if_second)
    weight = jnp.where(count_ref[0] > 3, 1.0, 0.0)
    acc[...] = acc[...] + weight * jnp.dot(win[place], tiles[0, 3], preferred_element_type=F32)

    arrived(gbuf, d_recv)
    out_ref[...] = (acc[...] + mul_t(flat(gbuf[...]), basis[0])).astype(out_ref.dtype)

    arrived(cbuf.at[0 : PEERS - 1], a_send)
    arrived(gbuf.at[0 : PEERS - 1], d_send)
    arrived(planes.at[0 : DEPTH - 1], z_send.at[0])
    for side in range(2):
        arrived(near_z.at[side], z_send.at[1 + side])
        arrived(quad_z.at[side], z_send.at[3 + side])
    arrived(win.at[0:7], n_send.at[0])

    @pl.when(has_beyond)
    def _():
        arrived(ask, n_send.at[3])
        arrived(chosen, n_send.at[1])

    @pl.when(sends_edge)
    def _():
        arrived(win.at[EDGE], n_send.at[2])


def per_device(points_x, leaf_basis, near_tiles, near_cols, near_count, transfer, coupling, couple_mask):
    vectors, points = points_x.shape
    rank = leaf_basis.shape[2]
    masks = jnp.transpose(couple_mask, (0, 2, 1))
    operands = (points_x, leaf_basis, near_tiles, transfer, coupling, near_cols, masks)
    hbm = pl.BlockSpec(memory_space=pltpu.HBM)
    block = (ROWS, rank)
    dma = pltpu.SemaphoreType.DMA
    return pl.pallas_call(
        kernel,
        out_shape=jax.ShapeDtypeStruct((vectors, points), BF16),
        in_specs=[pl.BlockSpec(memory_space=pltpu.SMEM)] + [hbm] * 7,
        out_specs=pl.BlockSpec(memory_space=pltpu.VMEM),
        scratch_shapes=[
            pltpu.VMEM((10, vectors, points), BF16),
            pltpu.VMEM(leaf_basis.shape, BF16),
            pltpu.VMEM(near_tiles.shape, BF16),
            pltpu.VMEM(transfer.shape, BF16),
            pltpu.VMEM(coupling.shape, BF16),
            pltpu.SMEM(masks.shape, jnp.int32),
            pltpu.SMEM(near_cols.shape, jnp.int32),
            pltpu.VMEM((PEERS,) + block, BF16),
            pltpu.VMEM((PEERS,) + block, BF16),
            pltpu.VMEM((15,) + block, BF16),
            pltpu.VMEM((2, 14) + block, BF16),
            pltpu.VMEM((2, 2) + block, BF16),
            pltpu.VMEM((DEPTH,) + block, BF16),
            pltpu.VMEM((PLANE,) + block, BF16),
            pltpu.VMEM((PEERS,) + block, BF16),
            pltpu.VMEM((vectors, points), F32),
            pltpu.VMEM((PLANE * ROWS, rank), F32),
            pltpu.VMEM((4 * rank, rank), BF16),
            pltpu.VMEM((8 * rank, rank), BF16),
            pltpu.VMEM((6 * rank, rank), BF16),
            pltpu.VMEM((rank, 6 * rank), BF16),
            pltpu.VMEM((8, 128), F32),
            pltpu.VMEM((8, 128), F32),
            pltpu.VMEM((vectors, points), BF16),
            dma((7,)), dma(()), dma(()), dma((5,)), dma((5,)), dma(()), dma(()), dma((4,)), dma((10,)), pltpu.SemaphoreType.REGULAR,
        ],
        compiler_params=pltpu.CompilerParams(
            collective_id=0, has_side_effects=True, vmem_limit_bytes=48 * 1024 * 1024
        ),
    )(near_count, *(pltpu.with_memory_space_constraint(a, pltpu.HBM) for a in operands))


def solution(mesh):
    in_specs = (
        P(None, ("leaf", "level")),
        P(("leaf", "level"), None, None),
        P(("leaf", "level"), None, None, None),
        P(("leaf", "level"), None),
        P(("leaf", "level")),
        P(),
        P(),
        P(),
    )
    out_specs = P(None, ("leaf", "level"))
    return jax.shard_map(per_device, mesh=mesh, in_specs=in_specs, out_specs=out_specs, check_vma=False)
```

time: 52.3 us -> 38 us (0.73)
  local copies, waits for them, and re-layouts: 7.89 us -> 0.71 us
  Pallas kernels: 43.4 us -> 36.5 us
    unnamed x15 -> x1, local copies, waits for them, and re-layouts: 7.89 us -> 0.71 us
    pallas_call x1, Pallas kernels: 43.4 us -> 36.5 us  [per_device(): pl.pallas_call(kernel, out_shape=jax.ShapeDtypeStruct((vectors, points),...]
where the time goes in v2:
time: 38 us; the launch traced here: 37.9 us
  Pallas kernels  36.5 us (96%)
  local copies, waits for them, and re-layouts  0.71 us (2%)
  between operations  0.66 us (2%)
    pallas_call x1, Pallas kernels, per_device(): pl.pallas_call(kernel, out_shape=jax.ShapeDtypeStruct((vectors, points),...  36.5 us

profile of v2, /device:TPU:1, one launch (start us, length us, event | category | flops | bytes accessed | tf_op | source)
XLA Modules:
  0.0 37.9 jit_solution(11286205706742239763)
XLA Ops:
  0.7 36.5 %shard_map.82 = bf16[256,512]{1,0:T(8,128)(2,1)S(1)} custom-call(s32[1]{0:T(128)S(6)} %copy.10.count_ref, bf16[256,512]{1,0:T(8,128)(2,1)} %x_hbm.1, bf16[1,512,256]{2,1,0:T(8,128)(2,1)} %basis_hbm.1, bf16[1,4,512,512]{3,2,1,0:T(8,128)(2,1)} %tiles_hbm.1, bf16[2,256,256]{2,1,0:T(8,128)(2,1)} %transfer_hbm.1, bf16[6,2,256,256]{3,2,1,0:T(8,128)(2,1)} %coupling_hbm.1, ...), custom_call_target="tpu_custom_call" | custom-call | tf_op jit(solution)/shard_map/pallas_call | solution.py:443
  37.2 0.7 %copy.11 = bf16[256,512]{1,0:T(8,128)(2,1)} copy(bf16[256,512]{1,0:T(8,128)(2,1)S(1)} %shard_map.82) | data formatting | bytes 524288

commit v3 on v2

--- a/solution.py
+++ b/solution.py
@@ -14,7 +14,7 @@
 DEPTH = 16
 GROUPS = PLANE * DEPTH
 ROWS = 8
-EARLY = 6
+EARLY = 5
 SEL, EDGE = 8, 9
 
 REACH = (0, 1, 2, 1)
@@ -22,7 +22,6 @@
     ((dx, dy, dc) for dx in range(4) for dy in range(4) for dc in range(2) if (dx, dy, dc) != (0, 0, 0)),
     key=lambda s: -(REACH[s[0]] + REACH[s[1]]),
 )
-DEPTH_STEPS = sorted(range(1, DEPTH), key=lambda s: -min(s, DEPTH - s))
 
 
 def flat(blocks):
@@ -52,9 +51,9 @@
     count_ref, x_hbm, basis_hbm, tiles_hbm, transfer_hbm, coupling_hbm, cols_hbm, mask_hbm,
     out_ref,
     win, basis, tiles, trans, coup, mask_ref, cols_ref,
-    cbuf, abuf, tree, near_z, quad_z, planes, fbuf, gbuf, acc, low,
+    cbuf, abuf, tree, near_z, quad_z, planes, fbuf, gbuf, lbuf, lows, acc, plane_basis,
     two, three, ahead_mats, behind_mats, ask, asked, chosen,
-    load_sem, a_send, a_recv, z_send, z_recv, d_send, d_recv, n_send, n_recv, above_sem,
+    load_sem, a_send, a_recv, z_send, z_recv, d_send, d_recv, l_send, l_recv, n_send, n_recv, above_sem, next_sem,
 ):
     g = lax.axis_index("leaf")
     x = lax.axis_index("level")
@@ -68,7 +67,9 @@
     partner_g = g + 1 - 2 * core
     beyond_g = (g + 2 * core - 1 + GROUPS) % GROUPS
     has_beyond = (g > 0) & (g < GROUPS - 1)
-    at_edge = x == core * (MEMBERS - 1)
+    edge_x = core * (MEMBERS - 1)
+    wants_edge = has_beyond & (x == edge_x)
+    sends_edge = has_beyond & (x == MEMBERS - 1 - edge_x)
     x_up, x_down, x_far = (x + 1) % MEMBERS, (x + 3) % MEMBERS, (x + 2) % MEMBERS
 
     def load(k, src, dst):
@@ -103,15 +104,10 @@
     for step in PEER_STEPS:
         other_gp, other_x = plane_peer(step)
         pl.semaphore_signal(barrier, inc=1, device_id=(base_g + other_gp, other_x), device_id_type=MESH)
-    edge_x = (MEMBERS - 1) * (1 - core)
 
     @pl.when(has_beyond)
     def _():
         pl.semaphore_signal(barrier, inc=1, device_id=(beyond_g, x), device_id_type=MESH)
-
-    @pl.when(has_beyond & at_edge)
-    def _():
-        pl.semaphore_signal(barrier, inc=1, device_id=(beyond_g, edge_x), device_id_type=MESH)
 
     def arrived(ref, sem):
         pltpu.make_async_copy(ref, ref, sem).wait()
@@ -129,12 +125,22 @@
         win[SEL] = jnp.zeros(win.shape[1:], BF16)
         win[EDGE] = jnp.zeros(win.shape[1:], BF16)
 
+    for distance, far in ((1, near_z), (2, quad_z)):
+
+        @pl.when(z < distance)
+        def _():
+            far[0] = jnp.zeros(far.shape[1:], BF16)
+
+        @pl.when(z >= DEPTH - distance)
+        def _():
+            far[1] = jnp.zeros(far.shape[1:], BF16)
+
     load_cols.wait()
     extra = cols_ref[0, 3]
     wanted = jnp.where(core == 0, extra, extra - 2 * MEMBERS)
     ask[...] = jnp.broadcast_to(wanted.astype(F32), ask.shape)
 
-    greeted = PEERS - 1 + z + jnp.where(has_beyond, 1, 0) + jnp.where(has_beyond & at_edge, 1, 0)
+    greeted = PEERS - 1 + z + jnp.where(has_beyond, 1, 0)
     pl.semaphore_wait(barrier, greeted)
 
     def greet_below(plane, carry):
@@ -142,6 +148,11 @@
         return carry
 
     lax.fori_loop(0, z, greet_below, 0)
+    for distance in (1, 2):
+
+        @pl.when(z >= distance)
+        def _():
+            pl.semaphore_signal(next_sem.at[distance - 1], inc=1, device_id=(g - distance * PLANE, x), device_id_type=MESH)
 
     def near_copy(src, dst, where, send, recv):
         return pltpu.make_async_remote_copy(
@@ -191,8 +202,7 @@
         three[4 * rank * upper : 4 * rank * (upper + 1)] = mul(two[...], trans[upper]).astype(BF16)
 
     sel_copy = near_copy(chosen, win.at[SEL], (beyond_g, x), 1, 5)
-    edge_copy = near_copy(win.at[x], win.at[EDGE], (beyond_g, edge_x), 2, 6)
-    sends_edge = has_beyond & at_edge
+    edge_copy = near_copy(win.at[edge_x], win.at[EDGE], (beyond_g, x), 2, 6)
     lanes = ask.shape[1]
 
     def relay():
@@ -202,6 +212,11 @@
         near_copy(last(x_up), last(x_up), (g, x_down), 0, 3).start()
         arrived(last(x_down), n_recv.at[8])
         arrived(first(x_up), n_recv.at[9])
+
+        @pl.when(sends_edge)
+        def _():
+            edge_copy.start()
+
         near_copy(win.at[x_down], win.at[4 + x_down], (partner_g, x), 0, 4).start()
         near_copy(win.at[x_up], win.at[4 + x_up], (partner_g, x), 0, 4).start()
 
@@ -223,10 +238,6 @@
                 chosen[:, at : at + lanes] = total.reshape(chosen.shape[0], lanes).astype(BF16)
             sel_copy.start()
 
-        @pl.when(sends_edge)
-        def _():
-            edge_copy.start()
-
     arrived(abuf, a_recv)
     rows = flat(abuf[...])
     share_rows = PLANE * ROWS
@@ -234,20 +245,19 @@
     in_line = jnp.concatenate([piece(tops, k) for k in range(PLANE)], axis=1)
     tree[14] = mul(in_line, three[...]).astype(BF16)
 
-    @pl.when(z < EARLY)
-    def _():
-        relay()
-
-    @pl.when(z < DEPTH - 1)
-    def _():
-        pl.semaphore_wait(above_sem, DEPTH - 1 - z)
-
-    for step in DEPTH_STEPS:
+    def send_plane(plane, carry):
         pltpu.make_async_remote_copy(
             src_ref=tree.at[14], dst_ref=planes.at[z], send_sem=z_send.at[0], recv_sem=z_recv.at[0],
-            device_id=z_peer(step), device_id_type=MESH,
+            device_id=(plane * PLANE + gp, x), device_id_type=MESH,
         ).start()
+        return carry
+
+    lax.fori_loop(0, z, send_plane, 0)
     pltpu.make_async_copy(tree.at[14], planes.at[z], z_recv.at[0]).start()
+
+    @pl.when(z >= EARLY)
+    def _():
+        share()
 
     def join(parts):
         count = parts.shape[0] // (2 * ROWS)
@@ -262,20 +272,23 @@
         blocks = part.shape[0] // ROWS
         tree[at : at + blocks] = part.reshape(blocks, ROWS, rank).astype(BF16)
         at += blocks
-    for side, step in ((0, 1), (1, DEPTH - 1)):
-        pltpu.make_async_remote_copy(
-            src_ref=tree.at[0:14], dst_ref=near_z.at[side], send_sem=z_send.at[1 + side],
-            recv_sem=z_recv.at[1 + side], device_id=z_peer(step), device_id_type=MESH,
-        ).start()
-    for side, step in ((0, 2), (1, DEPTH - 2)):
-        pltpu.make_async_remote_copy(
-            src_ref=tree.at[12:14], dst_ref=quad_z.at[side], send_sem=z_send.at[3 + side],
-            recv_sem=z_recv.at[3 + side], device_id=z_peer(step), device_id_type=MESH,
-        ).start()
-
-    @pl.when(z >= EARLY)
-    def _():
-        share()
+
+    def send_tree(side, step, blocks, target, k):
+        return pltpu.make_async_remote_copy(
+            src_ref=blocks, dst_ref=target.at[side], send_sem=z_send.at[k + side],
+            recv_sem=z_recv.at[k + side], device_id=z_peer(step), device_id_type=MESH,
+        )
+
+    tree_up, tree_down = (send_tree(k, s, tree.at[0:14], near_z, 1) for k, s in ((0, 1), (1, DEPTH - 1)))
+    quad_up, quad_down = (send_tree(k, s, tree.at[12:14], quad_z, 3) for k, s in ((0, 2), (1, DEPTH - 2)))
+
+    @pl.when(z >= 1)
+    def _():
+        tree_down.start()
+
+    @pl.when(z >= 2)
+    def _():
+        quad_down.start()
 
     load_coup.wait()
     down_two = two[pl.ds(pl.multiple_of((z % 4) * rank, rank), rank), :]
@@ -290,14 +303,34 @@
         ahead_mats[at : at + rank, :] = coup[3, pick]
         behind_mats[:, at : at + rank] = coup[3, pick]
 
+    plane_basis[...] = mul(basis[0], three[pl.ds(pl.multiple_of(gp * rank, rank), rank), :]).astype(BF16)
+
     load_tiles.wait()
     acc[...] = jnp.dot(win[x], tiles[0, 0], preferred_element_type=F32)
 
+    @pl.when(z < EARLY)
+    def _():
+        relay()
+
+    for distance, copy in ((1, tree_up), (2, quad_up)):
+
+        @pl.when(z < DEPTH - distance)
+        def _():
+            pl.semaphore_wait(next_sem.at[distance - 1], 1)
+            copy.start()
+
+    def reach_above():
+        @pl.when(z < DEPTH - 1)
+        def _():
+            pl.semaphore_wait(above_sem, DEPTH - 1 - z)
+
+        lax.fori_loop(z + 1, DEPTH, send_plane, 0)
+
     @pl.when(z >= EARLY)
     def _():
+        reach_above()
         relay()
 
-    relay_far()
     load_mask.wait()
 
     def flag(level, pick, index, valid):
@@ -336,10 +369,31 @@
             parts += [piece(lower, k), piece(upper, k)]
         return jnp.concatenate(parts, axis=0)
 
-    for side in range(2):
-        arrived(near_z.at[side], z_recv.at[1 + side])
-        arrived(quad_z.at[side], z_recv.at[3 + side])
-    low[...] = split(split(low_level(2, 2, 12)) + low_level(1, 4, 8)) + low_level(0, 8, 0)
+    for distance, far, k in ((1, near_z, 1), (2, quad_z, 3)):
+
+        @pl.when(z >= distance)
+        def _():
+            arrived(far.at[0], z_recv.at[k])
+
+        @pl.when(z < DEPTH - distance)
+        def _():
+            arrived(far.at[1], z_recv.at[k + 1])
+
+    low = split(split(low_level(2, 2, 12)) + low_level(1, 4, 8)) + low_level(0, 8, 0)
+    lbuf[...] = low.reshape(lbuf.shape).astype(BF16)
+    for step in PEER_STEPS:
+        other_gp, other_x = plane_peer(step)
+        pltpu.make_async_remote_copy(
+            src_ref=lbuf.at[other_gp], dst_ref=lows.at[me], send_sem=l_send, recv_sem=l_recv,
+            device_id=(base_g + other_gp, other_x), device_id_type=MESH,
+        ).start()
+    pltpu.make_async_copy(lbuf.at[gp], lows.at[me], l_recv).start()
+
+    @pl.when(z < EARLY)
+    def _():
+        reach_above()
+
+    relay_far()
 
     arrived(planes, z_recv.at[0])
     pair, quad = z // 2, z // 4
@@ -374,21 +428,19 @@
         behind += other
     field = mul(jnp.concatenate(ahead, axis=1), ahead_mats[...])
     field = field + mul_t(jnp.concatenate(behind, axis=1), behind_mats[...])
-    spread = mul_t(field, three[...])
-    spread = jnp.concatenate([spread[:, rank * k : rank * (k + 1)] for k in range(PLANE)], axis=0)
-    fbuf[...] = (spread + low[...]).reshape(fbuf.shape).astype(BF16)
+    fbuf[...] = field.astype(BF16)
 
     for step in PEER_STEPS:
         other_gp, other_x = plane_peer(step)
         pltpu.make_async_remote_copy(
-            src_ref=fbuf.at[other_gp], dst_ref=gbuf.at[me], send_sem=d_send, recv_sem=d_recv,
+            src_ref=fbuf, dst_ref=gbuf.at[me], send_sem=d_send, recv_sem=d_recv,
             device_id=(base_g + other_gp, other_x), device_id_type=MESH,
         ).start()
-    pltpu.make_async_copy(fbuf.at[gp], gbuf.at[me], d_recv).start()
+    pltpu.make_async_copy(fbuf, gbuf.at[me], d_recv).start()
 
     arrived(win.at[4:8], n_recv.at[4])
 
-    @pl.when(sends_edge)
+    @pl.when(wants_edge)
     def _():
         arrived(win.at[EDGE], n_recv.at[6])
 
@@ -411,15 +463,26 @@
     weight = jnp.where(count_ref[0] > 3, 1.0, 0.0)
     acc[...] = acc[...] + weight * jnp.dot(win[place], tiles[0, 3], preferred_element_type=F32)
 
+    arrived(lows, l_recv)
+    acc[...] = acc[...] + mul_t(flat(lows[...]), basis[0])
+
     arrived(gbuf, d_recv)
-    out_ref[...] = (acc[...] + mul_t(flat(gbuf[...]), basis[0])).astype(out_ref.dtype)
+    out_ref[...] = (acc[...] + mul_t(flat(gbuf[...]), plane_basis[...])).astype(out_ref.dtype)
 
     arrived(cbuf.at[0 : PEERS - 1], a_send)
     arrived(gbuf.at[0 : PEERS - 1], d_send)
+    arrived(lows.at[0 : PEERS - 1], l_send)
     arrived(planes.at[0 : DEPTH - 1], z_send.at[0])
-    for side in range(2):
-        arrived(near_z.at[side], z_send.at[1 + side])
-        arrived(quad_z.at[side], z_send.at[3 + side])
+    for distance, far, k in ((1, near_z, 1), (2, quad_z, 3)):
+
+        @pl.when(z < DEPTH - distance)
+        def _():
+            arrived(far.at[0], z_send.at[k])
+
+        @pl.when(z >= distance)
+        def _():
+            arrived(far.at[1], z_send.at[k + 1])
+
     arrived(win.at[0:7], n_send.at[0])
 
     @pl.when(has_beyond)
@@ -459,10 +522,12 @@
             pltpu.VMEM((2, 14) + block, BF16),
             pltpu.VMEM((2, 2) + block, BF16),
             pltpu.VMEM((DEPTH,) + block, BF16),
+            pltpu.VMEM(block, BF16),
+            pltpu.VMEM((PEERS,) + block, BF16),
             pltpu.VMEM((PLANE,) + block, BF16),
             pltpu.VMEM((PEERS,) + block, BF16),
             pltpu.VMEM((vectors, points), F32),
-            pltpu.VMEM((PLANE * ROWS, rank), F32),
+            pltpu.VMEM((points, rank), BF16),
             pltpu.VMEM((4 * rank, rank), BF16),
             pltpu.VMEM((8 * rank, rank), BF16),
             pltpu.VMEM((6 * rank, rank), BF16),
@@ -470,7 +535,8 @@
             pltpu.VMEM((8, 128), F32),
             pltpu.VMEM((8, 128), F32),
             pltpu.VMEM((vectors, points), BF16),
-            dma((7,)), dma(()), dma(()), dma((5,)), dma((5,)), dma(()), dma(()), dma((4,)), dma((10,)), pltpu.SemaphoreType.REGULAR,
+            dma((7,)), dma(()), dma(()), dma((5,)), dma((5,)), dma(()), dma(()), dma(()), dma(()), dma((4,)), dma((10,)), pltpu.SemaphoreType.REGULAR,
+            pltpu.SemaphoreType.REGULAR((2,)),
         ],
         compiler_params=pltpu.CompilerParams(
             collective_id=0, has_side_effects=True, vmem_limit_bytes=48 * 1024 * 1024

time: 38 us -> 36.1 us (0.950)
  Pallas kernels: 36.5 us -> 34.6 us
    pallas_call x1, Pallas kernels: 36.5 us -> 34.6 us  [per_device(): pl.pallas_call(kernel, out_shape=jax.ShapeDtypeStruct((vectors, points),...]
where the time goes in v3:
time: 36.1 us; the launch traced here: 36 us
  Pallas kernels  34.6 us (96%)
  local copies, waits for them, and re-layouts  0.71 us (2%)
  between operations  0.66 us (2%)
    pallas_call x1, Pallas kernels, per_device(): pl.pallas_call(kernel, out_shape=jax.ShapeDtypeStruct((vectors, points),...  34.6 us

profile of v3, /device:TPU:1, one launch (start us, length us, event | category | flops | bytes accessed | tf_op | source)
XLA Modules:
  0.0 36.0 jit_solution(12271837853323585425)
XLA Ops:
  0.7 34.6 %shard_map.82 = bf16[256,512]{1,0:T(8,128)(2,1)S(1)} custom-call(s32[1]{0:T(128)S(6)} %copy.10.count_ref, bf16[256,512]{1,0:T(8,128)(2,1)} %x_hbm.1, bf16[1,512,256]{2,1,0:T(8,128)(2,1)} %basis_hbm.1, bf16[1,4,512,512]{3,2,1,0:T(8,128)(2,1)} %tiles_hbm.1, bf16[2,256,256]{2,1,0:T(8,128)(2,1)} %transfer_hbm.1, bf16[6,2,256,256]{3,2,1,0:T(8,128)(2,1)} %coupling_hbm.1, ...), custom_call_target="tpu_custom_call" | custom-call | tf_op jit(solution)/shard_map/pallas_call | solution.py:506
  35.3 0.7 %copy.11 = bf16[256,512]{1,0:T(8,128)(2,1)} copy(bf16[256,512]{1,0:T(8,128)(2,1)S(1)} %shard_map.82) | data formatting | bytes 524288

commit v4 on v3

--- a/solution.py
+++ b/solution.py
@@ -330,6 +330,7 @@
     def _():
         reach_above()
         relay()
+        relay_far()
 
     load_mask.wait()
 
@@ -392,8 +393,8 @@
     @pl.when(z < EARLY)
     def _():
         reach_above()
-
-    relay_far()
+        relay_far()
+
 
     arrived(planes, z_recv.at[0])
     pair, quad = z // 2, z // 4

time: 36.1 us -> 36.1 us (level)
  no operation moved by 1% of the time
where the time goes in v4:
time: 36.1 us; the launch traced here: 36 us
  Pallas kernels  34.6 us (96%)
  local copies, waits for them, and re-layouts  0.71 us (2%)
  between operations  0.66 us (2%)
    pallas_call x1, Pallas kernels, per_device(): pl.pallas_call(kernel, out_shape=jax.ShapeDtypeStruct((vectors, points),...  34.6 us

profile of v4, /device:TPU:1, one launch (start us, length us, event | category | flops | bytes accessed | tf_op | source)
XLA Modules:
  0.0 36.0 jit_solution(14720872771655227262)
XLA Ops:
  0.7 34.6 %shard_map.82 = bf16[256,512]{1,0:T(8,128)(2,1)S(1)} custom-call(s32[1]{0:T(128)S(6)} %copy.10.count_ref, bf16[256,512]{1,0:T(8,128)(2,1)} %x_hbm.1, bf16[1,512,256]{2,1,0:T(8,128)(2,1)} %basis_hbm.1, bf16[1,4,512,512]{3,2,1,0:T(8,128)(2,1)} %tiles_hbm.1, bf16[2,256,256]{2,1,0:T(8,128)(2,1)} %transfer_hbm.1, bf16[6,2,256,256]{3,2,1,0:T(8,128)(2,1)} %coupling_hbm.1, ...), custom_call_target="tpu_custom_call" | custom-call | tf_op jit(solution)/shard_map/pallas_call | solution.py:507
  35.3 0.7 %copy.11 = bf16[256,512]{1,0:T(8,128)(2,1)} copy(bf16[256,512]{1,0:T(8,128)(2,1)S(1)} %shard_map.82) | data formatting | bytes 524288
